TPU v7x, 32 devices: a whole 2x2x4 slice. The times are simulated.
32 devices in a mesh: row: 16 (over z, y, core), col: 2 (over x).
Axes of the slice: x: 2, y: 2, z: 4, core: 2. Of those that a mesh axis runs over, the one named last changes fastest.
Arguments:
- x_in: bfloat16 [2, 16384, 768], P(None, 'row', 'col'), may hold values from -6 to 6
- span_start: int32 [2, 16, 2], P(None, 'row'), may hold values from 0 to 768, as said below
- span_kind: int32 [2, 16, 2], P(None, 'row'), may hold values from 0 to 1
- ln1_gain: float32 [768], P('col'), may hold values from 0.5 to 1.5
- ln1_bias: float32 [768], P('col'), may hold values from -3 to 3
- w_qkv: bfloat16 [768, 3, 768], P('row', None, 'col'), may hold values from -0.3125 to 0.3125
- b_query: float32 [768], P('col'), may hold values from -3 to 3
- b_value: float32 [768], P('col'), may hold values from -3 to 3
- w_out: bfloat16 [768, 768], P('col', 'row'), may hold values from -0.875 to 0.875
- b_out: float32 [768], P('col'), may hold values from -3 to 3
- ln2_gain: float32 [768], P('col'), may hold values from 0.5 to 1.5
- ln2_bias: float32 [768], P('col'), may hold values from -3 to 3
- w_fc: bfloat16 [768, 3072], P('row', 'col'), may hold values from -0.21875 to 0.21875
- b_fc: float32 [3072], P('col'), may hold values from -3 to 3
- w_proj: bfloat16 [3072, 768], P('col', 'row'), may hold values from -0.15625 to 0.15625
- b_proj: float32 [768], P('col'), may hold values from -3 to 3
- cotangent: bfloat16 [2, 16384, 768], P(None, 'row', 'col'), may hold values from -6 to 6
Outputs:
- layer_out: bfloat16 [2, 16384, 768], P(None, 'row', 'col')
- grad_input: bfloat16 [2, 16384, 768], P(None, 'row', 'col')
- g_ln1_gain: float32 [768], P('col')
- g_ln1_bias: float32 [768], P('col')
- g_w_qkv: float32 [768, 3, 768], P('row', None, 'col')
- g_b_query: float32 [768], P('col')
- g_b_value: float32 [768], P('col')
- g_w_out: float32 [768, 768], P('col', 'row')
- g_b_out: float32 [768], P('col')
- g_ln2_gain: float32 [768], P('col')
- g_ln2_bias: float32 [768], P('col')
- g_w_fc: float32 [768, 3072], P('row', 'col')
- g_b_fc: float32 [3072], P('col')
- g_w_proj: float32 [3072, 768], P('col', 'row')
- g_b_proj: float32 [768], P('col')
Inputs may be any that keep to these rules, and one draw needn't show every extreme that they name: `span_start`: span j of a sequence starts within the j-th of 2 equal parts of the sequence and ends within it, so spans never intersect.
All inputs are finite; a program needn't handle non-finite values.
Results may differ from a plain program's by a relative error of at most 0.017.
Values may be sent and summed in bfloat16 or wider, within the bound.
A program may use at most 192 MiB of HBM per device.

v0:
```python
from functools import partial

import jax
import jax.numpy as jnp
from jax import lax
from jax.experimental import pallas as pl
from jax.experimental.pallas import tpu as pltpu
from jax.sharding import PartitionSpec as P

HEAD = 64
IMG = 256
epsilon = 1e-05
bf16 = jnp.bfloat16
f32 = jnp.float32
GELU_A = 0.7978845608028654
GELU_B = 0.044715
PAIR = 2 * HEAD


def nn(a, b):
    return lax.dot_general(a, b, (((1,), (0,)), ((), ())), preferred_element_type=f32)


def nt(a, b):
    return lax.dot_general(a, b, (((1,), (1,)), ((), ())), preferred_element_type=f32)


def tn(a, b):
    return lax.dot_general(a, b, (((0,), (0,)), ((), ())), preferred_element_type=f32)


def half_bias(start, kind, part, half):
    base = part * half
    rows = lax.broadcasted_iota(jnp.int32, (half, half), 0) + base
    cols = lax.broadcasted_iota(jnp.int32, (half, half), 1) + base
    first = jnp.where(kind == 1, start, 4 * half)
    joined = (rows >= first) & (rows < first + IMG) & (cols >= first) & (cols < first + IMG)
    return jnp.where((cols <= rows) | joined, 0.0, -1e30).astype(f32)


def lane_masks(rows):
    lane = lax.broadcasted_iota(jnp.int32, (rows, PAIR), 1)
    return lane < HEAD


def attend_pair(qkv_ref, o_ref, p_ref, inv_ref, bias_ref):
    half = qkv_ref.shape[0] // 2
    q_ref, k_ref, v_ref = (qkv_ref.at[:, i * PAIR : (i + 1) * PAIR] for i in range(3))
    low = lane_masks(half)
    for part in range(2):
        rows = slice(part * half, (part + 1) * half)
        q = q_ref[rows, :] * jnp.asarray(0.125, bf16)
        zero = jnp.zeros_like(q)
        outs = []
        invs = []
        for head in range(2):
            mine = low if head == 0 else jnp.logical_not(low)
            qh = jnp.where(mine, q, zero)
            own = nt(qh, k_ref[rows, :]) + bias_ref[part]
            largest = jnp.max(own, axis=1, keepdims=True)
            if part == 1:
                before = nt(qh, k_ref[:half, :])
                largest = jnp.maximum(largest, jnp.max(before, axis=1, keepdims=True))
            own = jnp.exp(own - largest)
            total = jnp.sum(own, axis=1, keepdims=True)
            own = own.astype(bf16)
            p_ref[:, (3 * head + 2 * part) * half : (3 * head + 2 * part + 1) * half] = own
            out = nn(own, v_ref[rows, :])
            if part == 1:
                before = jnp.exp(before - largest)
                total = total + jnp.sum(before, axis=1, keepdims=True)
                before = before.astype(bf16)
                p_ref[:, (3 * head + 1) * half : (3 * head + 2) * half] = before
                out = out + nn(before, v_ref[:half, :])
            inv = 1.0 / total
            outs.append(out * inv)
            invs.append(inv)
        o_ref[rows, :] = jnp.where(low, outs[0], outs[1]).astype(bf16)
        inv_ref[rows, :] = jnp.where(low, invs[0], invs[1])


def attend_forward_kernel(span_ref, qkv_ref, o_ref, p_ref, inv_ref, bias_ref):
    half = qkv_ref.shape[0] // 2

    @pl.when(pl.program_id(0) == 0)
    def _():
        for part in range(2):
            bias_ref[part] = half_bias(span_ref[0, part], span_ref[1, part], part, half)

    attend_pair(qkv_ref, o_ref, p_ref.at[0], inv_ref, bias_ref)


def attend_forward(packed, spans):
    length = packed.shape[0]
    width = packed.shape[1] // 3
    pairs = width // PAIR
    half = length // 2
    return pl.pallas_call(
        attend_forward_kernel,
        grid=(pairs,),
        in_specs=[
            pl.BlockSpec(memory_space=pltpu.SMEM),
            pl.BlockSpec((length, 3 * PAIR), lambda j: (0, j)),
        ],
        out_specs=[
            pl.BlockSpec((length, PAIR), lambda j: (0, j)),
            pl.BlockSpec((1, half, 6 * half), lambda j: (j, 0, 0)),
            pl.BlockSpec((length, PAIR), lambda j: (0, j)),
        ],
        out_shape=[
            jax.ShapeDtypeStruct((length, width), bf16),
            jax.ShapeDtypeStruct((pairs, half, 6 * half), bf16),
            jax.ShapeDtypeStruct((length, width), f32),
        ],
        scratch_shapes=[pltpu.VMEM((2, half, half), f32)],
        compiler_params=pltpu.CompilerParams(vmem_limit_bytes=60 << 20),
        cost_estimate=pl.CostEstimate(
            flops=4 * 3 * half * half * width * 4, bytes_accessed=24 << 20, transcendentals=3 * half * half * 12
        ),
        name="attend_forward",
    )(spans, packed)


def attend_back_pair(qkv_ref, o_ref, p_ref, inv_ref, g_ref, sum_ref):
    length = qkv_ref.shape[0]
    half = length // 2
    low = lane_masks(half)
    q_ref, k_ref, v_ref = (qkv_ref.at[:, i * PAIR : (i + 1) * PAIR] for i in range(3))
    dks = [None, None]
    dvs = [None, None]
    dqs = []

    def add(total, part, value):
        total[part] = value if total[part] is None else total[part] + value

    for part in range(2):
        rows = slice(part * half, (part + 1) * half)
        inv = inv_ref[rows, :]
        g = g_ref[rows, :].astype(f32) * inv
        scaled = g * o_ref[rows, :].astype(f32)
        q = q_ref[rows, :]
        gb = g.astype(bf16)
        zero = jnp.zeros_like(gb)
        dq = None
        for head in range(2):
            mine = low if head == 0 else jnp.logical_not(low)
            gh = jnp.where(mine, gb, zero)
            qh = jnp.where(mine, q, zero)
            rowdot = jnp.sum(jnp.where(mine, scaled, 0.0), axis=1, keepdims=True)
            for kpart in range(part + 1):
                krows = slice(kpart * half, (kpart + 1) * half)
                at = (3 * head + part + kpart) * half
                p = p_ref[:, at : at + half]
                kh = jnp.where(mine, k_ref[krows, :], zero)
                dp = nt(gh, v_ref[krows, :])
                ds = (p.astype(f32) * (dp - rowdot)).astype(bf16)
                term = nn(ds, kh)
                dq = term if dq is None else dq + term
                add(dks, kpart, tn(ds, qh))
                add(dvs, kpart, tn(p, gh))
        dqs.append(dq)
    for which, (ref, values, scale) in enumerate(((q_ref, dqs, 0.125), (k_ref, dks, 0.125), (v_ref, dvs, 1.0))):
        total = None
        for part in range(2):
            value = (values[part] * scale).astype(bf16)
            ref[part * half : (part + 1) * half, :] = value
            term = jnp.sum(value.astype(f32), axis=0, keepdims=True)
            total = term if total is None else total + term
        if which != 1:
            sum_ref[which // 2] = total


def attend_backward_kernel(qkv_ref, o_ref, p_ref, inv_ref, g_ref, d_ref, sum_ref):
    d_ref[...] = qkv_ref[...]
    attend_back_pair(d_ref, o_ref, p_ref.at[0], inv_ref, g_ref, sum_ref.at[0])


def attend_backward(packed, attended, p, inv, grad_attended):
    length = packed.shape[0]
    width = packed.shape[1] // 3
    pairs = width // PAIR
    half = length // 2
    one = pl.BlockSpec((length, PAIR), lambda j: (0, j))
    three = pl.BlockSpec((length, 3 * PAIR), lambda j: (0, j))
    return pl.pallas_call(
        attend_backward_kernel,
        grid=(pairs,),
        in_specs=[three, one, pl.BlockSpec((1, half, 6 * half), lambda j: (j, 0, 0)), one, one],
        out_specs=[three, pl.BlockSpec((1, 2, 1, PAIR), lambda j: (j, 0, 0, 0))],
        out_shape=[
            jax.ShapeDtypeStruct(packed.shape, bf16),
            jax.ShapeDtypeStruct((pairs, 2, 1, PAIR), f32),
        ],
        compiler_params=pltpu.CompilerParams(vmem_limit_bytes=56 << 20),
        name="attend_backward",
    )(packed, attended, p, inv, grad_attended)


SWAP = [(0, 1), (1, 0)]


def swap(value):
    return lax.ppermute(value, "col", SWAP)


def ordered(mine, other, axis):
    first = lax.axis_index("col") == 0
    low = jnp.where(first, mine, other)
    high = jnp.where(first, other, mine)
    return jnp.concatenate([low, high], axis=axis)


def own_micro(halves):
    col = lax.axis_index("col")
    mine = lax.dynamic_index_in_dim(halves, col, 0, keepdims=False)
    other = swap(lax.dynamic_index_in_dim(halves, 1 - col, 0, keepdims=False))
    return ordered(mine, other, 1)


def back_micro(full):
    col = lax.axis_index("col")
    half = full.shape[1] // 2
    mine = lax.dynamic_slice_in_dim(full, col * half, half, 1)
    other = swap(lax.dynamic_slice_in_dim(full, (1 - col) * half, half, 1))
    first = col == 0
    return jnp.stack([jnp.where(first, mine, other), jnp.where(first, other, mine)])


G0_ORDERS = ("xzy", "xzy", "xyz")
REST_ORDERS = ("zxy", "zxy", "xyz")
MIDDLE_CUT = (5 / 15, 6 / 15)
GATHER_CUT = (4 / 12, 4 / 12)
REDUCE_CUT = (10 / 27, 11 / 27)


MESH = pl.DeviceIdType.MESH
DEPTH = 4
WAYS = ("up", "down", "y", "x", "core")
SIZES = {"z": DEPTH, "y": 2, "x": 2}


def row_of(z, y, core):
    return z * 4 + y * 2 + core


def my_place():
    row = lax.axis_index("row")
    return row // 4, (row // 2) % 2, row % 2, lax.axis_index("col")


def maybe(cond, act):
    if cond is None:
        act()
    else:
        pl.when(cond)(act)


def remote(src, dst, send, recv, device):
    return pltpu.make_async_remote_copy(
        src_ref=src, dst_ref=dst, send_sem=send, recv_sem=recv, device_id=device, device_id_type=MESH
    )


def greet(always, z, up, down):
    barrier = pltpu.get_barrier_semaphore()

    def hello(device):
        pl.semaphore_signal(barrier, inc=1, device_id=device, device_id_type=MESH)

    for device in always:
        hello(device)
    pl.when(z < DEPTH - 1)(lambda: hello(up))
    pl.when(z > 0)(lambda: hello(down))
    pl.semaphore_wait(
        barrier, len(always) + (z < DEPTH - 1).astype(jnp.int32) + (z > 0).astype(jnp.int32)
    )


def tree_rounds(order):
    rounds = {}
    for dz in (0, -1, 1, -2, 2, -3, 3):
        for dy in (0, 1):
            for dx in (0, 1):
                step = {"z": dz, "y": dy, "x": dx}
                via = None
                for axis in order:
                    if step[axis]:
                        via = axis
                onward = []
                open_now = via is None
                for axis in order:
                    if axis == via:
                        open_now = True
                    if not open_now:
                        continue
                    if axis == "z":
                        onward += ["up"] if dz <= 0 else []
                        onward += ["down"] if dz >= 0 else []
                    elif axis != via:
                        onward.append(axis)
                onward.append("core")
                rounds.setdefault(abs(dz) + dy + dx, []).append((dz, dy, dx, onward))
    return rounds


def pieces_of(widths, cuts):
    found = []
    for part in range(3):
        base = 0
        for weight, width in enumerate(widths):
            lo = max(base, cuts[part])
            hi = min(base + width, cuts[part + 1])
            if hi > lo:
                found.append((part, weight, lo - cuts[part], lo - base, hi - lo))
            base += width
    return found


class Gatherer:
    def __init__(self, place, shards, widths, cuts, orders, scratch):
        self.z, self.y, self.core, self.x = place
        z, y, core, x = place
        self.shards, self.widths = shards, widths
        self.by_pairs = len(scratch) == 4
        self.whole = scratch[0]
        self.bufs = [scratch[0].at[part] for part in range(3)] if self.by_pairs else scratch[:3]
        self.send, self.recv, self.local = scratch[-3:]
        self.near = {
            "up": (row_of(z + 1, y, core), x),
            "down": (row_of(z - 1, y, core), x),
            "y": (row_of(z, 1 - y, core), x),
            "x": (row_of(z, y, core), 1 - x),
            "core": (row_of(z, y, 1 - core), x),
        }
        self.has = {"up": z < DEPTH - 1, "down": z > 0}
        self.orders = orders
        self.pieces = pieces_of(widths, cuts)
        self.trees = [tree_rounds(order) for order in orders]

    @staticmethod
    def scratch_shapes(cuts, rows, by_pairs):
        dma = pltpu.SemaphoreType.DMA
        if by_pairs:
            bufs = [pltpu.VMEM((3, 2, 16, rows, 3 * PAIR), bf16)]
        else:
            bufs = [pltpu.VMEM((2, 16, rows, cuts[i + 1] - cuts[i]), bf16) for i in range(3)]
        return bufs + [
            dma((3, 5)),
            dma((3, 17)),
            dma((3, 6)),
        ]

    def loads(self):
        row = row_of(self.z, self.y, self.core)
        if self.by_pairs:
            return [
                pltpu.make_async_copy(
                    self.shards[0].at[which, :, pl.ds(part * PAIR, PAIR)],
                    self.bufs[part].at[self.x, row, :, pl.ds(which * PAIR, PAIR)],
                    self.local.at[which, part],
                )
                for part in range(3)
                for which in range(3)
            ]
        return [
            pltpu.make_async_copy(
                self.shards[weight].at[:, pl.ds(src, width)],
                self.bufs[part].at[self.x, row, :, pl.ds(at, width)],
                self.local.at[0, i],
            )
            for i, (part, weight, at, src, width) in enumerate(self.pieces)
        ]

    def copy(self, part, bz, by, bx, way):
        block = self.bufs[part].at[bx, row_of(bz, by, self.core)]
        slot = 16 if way == "core" else bx * 8 + bz * 2 + by
        return remote(
            block, block, self.send.at[part, WAYS.index(way)], self.recv.at[part, slot], self.near[way]
        )

    def all_of(self, part, count, way):
        blocks = self.bufs[part].at[0, pl.ds(0, count)]
        return remote(
            blocks, blocks, self.send.at[part, WAYS.index(way)], self.recv.at[part, 16], self.near[way]
        )

    def each(self, step, act, parts=(0, 1, 2)):
        for part in parts:
            for dz, dy, dx, onward in self.trees[part].get(step, []):
                bz, by, bx = self.z + dz, (self.y + dy) % 2, (self.x + dx) % 2
                cond = None if dz == 0 else ((bz >= 0) & (bz <= DEPTH - 1))
                maybe(cond, lambda: act(part, bz, by, bx, onward))

    def forward(self, step, parts=(0, 1, 2)):
        def act(part, bz, by, bx, onward):
            if step:
                self.copy(part, bz, by, bx, "y").wait_recv()
            for way in onward:
                maybe(self.has.get(way), lambda way=way: self.copy(part, bz, by, bx, way).start())

        self.each(step, act, parts)

    def arrive(self, parts=(0, 1, 2)):
        for part in parts:
            self.all_of(part, 16, "core").wait_recv()

    def drain(self):
        for part in range(3):
            count = 1
            for axis in self.orders[part]:
                if axis == "z":
                    for at in range(DEPTH):

                        def act(part=part, at=at, count=count):
                            if at < DEPTH - 1:
                                self.all_of(part, count * (at + 1), "up").wait_send()
                            if at > 0:
                                self.all_of(part, count * (DEPTH - at), "down").wait_send()

                        pl.when(self.z == at)(act)
                else:
                    self.all_of(part, count, axis).wait_send()
                count *= SIZES[axis]
            self.all_of(part, count, "core").wait_send()

    def stores(self, outs):
        return [
            pltpu.make_async_copy(
                self.bufs[part].at[side, :, :, pl.ds(at, width)],
                outs[weight].at[:, :, pl.ds(side * self.widths[weight] + src, width)],
                self.local.at[1 + side, i],
            )
            for i, (part, weight, at, src, width) in enumerate(self.pieces)
            for side in range(2)
        ]

    def weight(self, part, side, at, width):
        block = self.bufs[part][side, :, :, at : at + width]
        return block.reshape(-1, width)


def begin(copies):
    for copy in copies:
        copy.start()


def end(copies):
    for copy in copies:
        copy.wait()


FORWARD_ORDER = (0, 3, 1, 4, 2, 5)
ROWS = 256


def front_kernel(shape, *refs):
    w_qkv, w_out, w_fc, w_proj, x_in, cot, starts, kinds = refs[:8]
    vectors = refs[8:17]
    (
        o_qkv, o_out, o_fc, o_proj, o_x, o_cot, o_vec, o_packed, o_p, o_inv, o_att, o_normed, o_middle, o_second,
        o_active, o_slope,
    ) = refs[17:33]
    scr = refs[33:]
    place = my_place()
    z, y, core, x = place
    one, two, three = (
        Gatherer(place, shards, *shape["groups"][i], scr[6 * i - 2 * (i > 0) : 6 * i + 4])
        for i, shards in enumerate(([w_qkv], [w_out, w_fc], [w_proj]))
    )
    (
        xm, xo, cm, xf, n1, pk, big, ib, att, bias, mid, n2, shifts, s_x, r_x, s_c, r_c, s_v, r_v, s_in, s_pair, s_end,
    ) = scr[16:-9]
    vec_o = scr[-9:]
    length, half_width = xm.shape
    width = 2 * half_width
    half = length // 2
    blocks = length // ROWS
    to_x = one.near["x"]

    def x_copy(i):
        span = pl.ds(i * ROWS, ROWS)
        return remote(x_in.at[1 - x, span], xo.at[span], s_x.at[i], r_x.at[i], to_x)

    own_cols = pl.ds(pl.multiple_of(x * half_width, PAIR), half_width)

    def cot_copy(i):
        span = pl.ds(i * ROWS, ROWS)
        return remote(cot.at[1 - x, span], o_cot.at[span, own_cols], s_c.at[i], r_c.at[i], to_x)

    vec_at = [sum(shape["vectors"][:k]) for k in range(9)]
    vec_copies = [
        remote(vector, vec_o[k], s_v.at[k], r_v.at[k], to_x) for k, vector in enumerate(vectors)
    ]
    own_x = pltpu.make_async_copy(x_in.at[x], xm, s_in.at[0])
    own_cot = pltpu.make_async_copy(cot.at[x], cm, s_in.at[1])
    put_cot = pltpu.make_async_copy(cm, o_cot.at[:, own_cols], s_in.at[2])
    begin(one.loads())
    own_x.start()
    begin(two.loads())
    begin(three.loads())
    own_cot.start()
    greet([to_x, one.near["y"], one.near["core"]], z, one.near["up"], one.near["down"])
    begin(vec_copies)
    end(one.loads())
    one.forward(0)
    begin([x_copy(i) for i in range(blocks)])
    for part in range(2):
        bias[part] = half_bias(starts[x, 0, part], kinds[x, 0, part], part, half)
    one.forward(1)
    end(two.loads())
    end(three.loads())
    one.forward(2)
    two.forward(0)
    end(vec_copies)
    is_low = x == 0
    full = []
    for vector, brought, at, size in zip(vectors, vec_o, vec_at, shape["vectors"]):
        mine, other = vector[...].reshape(1, size), brought[...].reshape(1, size)
        low, high = jnp.where(is_low, mine, other), jnp.where(is_low, other, mine)
        o_vec[:, 2 * at : 2 * at + size] = low
        o_vec[:, 2 * at + size : 2 * at + 2 * size] = high
        full.append(slice(2 * at, 2 * at + 2 * size))
    own_x.wait()

    def norm(value, gain, shift):
        average = jnp.sum(value, axis=1, keepdims=True) / width
        square = jnp.sum(value * value, axis=1, keepdims=True) / width
        inverse = lax.rsqrt(square - average * average + epsilon)
        return ((value - average) * inverse * o_vec[:, full[gain]] + o_vec[:, full[shift]]).astype(bf16)

    def first_norm(i):
        span = slice(i * ROWS, (i + 1) * ROWS)
        x_copy(i).wait_recv()
        mine, other = xm[span, :], xo[span, :]
        xf[span, :half_width] = jnp.where(is_low, mine, other)
        xf[span, half_width:] = jnp.where(is_low, other, mine)
        n1[span, :] = norm(xf[span, :].astype(f32), 0, 1)

    one.forward(3)
    first_norm(0)
    first_norm(1)
    one.forward(4)
    first_norm(2)
    one.forward(5)
    first_norm(3)
    two.forward(1)
    to_x_out = pltpu.make_async_copy(xf, o_x, s_end.at[0])
    to_normed = pltpu.make_async_copy(n1, o_normed, s_end.at[1])
    begin([to_x_out, to_normed])

    def pair_puts(j, step):
        wide = pl.ds(pl.multiple_of(3 * PAIR * j, PAIR), 3 * PAIR)
        cols = pl.ds(pl.multiple_of(PAIR * j, PAIR), PAIR)
        return [
            pltpu.make_async_copy(pk.at[j], o_packed.at[:, wide], s_pair.at[0]),
            pltpu.make_async_copy(big.at[step], o_p.at[j], s_pair.at[1]),
            pltpu.make_async_copy(ib.at[j], o_inv.at[:, cols], s_pair.at[2]),
            pltpu.make_async_copy(att.at[j], o_att.at[:, cols], s_pair.at[3]),
        ]

    def serve_0():
        two.forward(2)
        one.arrive((1,))

    def serve_1():
        two.forward(3)
        three.forward(0)

    def serve_2():
        two.forward(4)
        cot_copy(0).start()
        one.arrive((2,))
        begin(one.stores([o_qkv]))

    def serve_3():
        two.forward(5)
        three.forward(1)
        cot_copy(1).start()
        own_cot.wait()
        put_cot.start()

    def serve_4():
        three.forward(2)
        cot_copy(2).start()

    def serve_5():
        three.forward(3)
        cot_copy(3).start()

    serves = (serve_0, serve_1, serve_2, serve_3, serve_4, serve_5)
    for j in range(6):
        for k, vector in ((0, 2), (2, 3)):
            cols = slice(full[vector].start + PAIR * j, full[vector].start + PAIR * (j + 1))
            shifts[j, :, k * PAIR : (k + 1) * PAIR] = o_vec[:, cols]
        shifts[j, :, PAIR : 2 * PAIR] = jnp.zeros((1, PAIR), f32)

    def pair(step, carry):
        part, side = step // 2, step % 2
        j = 3 * side + part
        weight = one.whole[part, side].reshape(width, 3 * PAIR)
        pk[j] = (nn(n1[...], weight) + shifts[j]).astype(bf16)
        attend_pair(pk.at[j], att.at[j], big.at[step], ib.at[j], bias)
        begin(pair_puts(j, step))
        for k, serve in enumerate(serves):
            pl.when(step == k)(serve)
        return carry

    one.arrive((0,))
    lax.fori_loop(0, 6, pair, 0)
    qkv_stores = one.stores([o_qkv])
    two.arrive()
    two_stores = two.stores([o_out, o_fc])
    begin(two_stores)
    out_pieces = [p for p in two.pieces if p[1] == 0]
    fc_pieces = [p for p in two.pieces if p[1] == 1]

    def second(i, carry):
        span = pl.ds(pl.multiple_of(i * ROWS, ROWS), ROWS)
        total = xf[span, :].astype(f32) + o_vec[:, full[4]]
        rows = jnp.concatenate([att[j, span, :] for j in range(6)], axis=1)
        for part, _, at, src, w in out_pieces:
            for side in range(2):
                cols = slice(side * half_width + src, side * half_width + src + w)
                total = total + nt(rows[:, cols], two.weight(part, side, at, w))
        mid[span, :] = total
        n2[span, :] = norm(total, 5, 6)
        return carry

    lax.fori_loop(0, blocks, second, 0)
    for step in range(6):
        end(pair_puts(3 * (step % 2) + step // 2, step))
    to_mid = pltpu.make_async_copy(mid, o_middle, s_end.at[3])
    to_second = pltpu.make_async_copy(n2, o_second, s_end.at[4])
    begin([to_mid, to_second])
    three.forward(4)
    ff_half = two.widths[1]
    puts = []
    for k, ((part, _, at, src, w), side) in enumerate([(p, side) for p in fc_pieces for side in range(2)]):
        cols = slice(side * ff_half + src, side * ff_half + src + w)
        b_cols = slice(full[7].start + cols.start, full[7].start + cols.stop)

        def block(i, carry):
            span = pl.ds(pl.multiple_of(i * ROWS, ROWS), ROWS)
            hidden = nn(n2[span, :], two.weight(part, side, at, w)) + o_vec[:, b_cols]
            squared = hidden * hidden
            tanh = jnp.tanh(hidden * (GELU_A + (GELU_A * GELU_B) * squared))
            gate = 0.5 + 0.5 * tanh
            here = pl.ds(pl.multiple_of((i % 2) * ROWS, ROWS), ROWS)
            big[i // 2, here, cols] = (hidden * gate).astype(bf16)
            inner = hidden * (GELU_A + (3.0 * GELU_A * GELU_B) * squared)
            big[2 + i // 2, here, cols] = (gate + inner * (0.5 - 0.5 * tanh * tanh)).astype(bf16)
            return carry

        lax.fori_loop(0, blocks, block, 0)
        now = [
            pltpu.make_async_copy(big.at[0:2, :, cols], o_active.at[:, :, cols], s_end.at[5 + 2 * k]),
            pltpu.make_async_copy(big.at[2:4, :, cols], o_slope.at[:, :, cols], s_end.at[6 + 2 * k]),
        ]
        begin(now)
        puts += now
        if k == 1:
            three.forward(5)
    three.arrive()
    three_stores = three.stores([o_proj])
    begin(three_stores)
    one.drain()
    two.drain()
    three.drain()
    for i in range(blocks):
        x_copy(i).wait_send()
    for i in range(blocks):
        cot_copy(i).wait()
    end([put_cot, to_x_out, to_normed, to_mid, to_second] + puts)
    end(qkv_stores)
    end(two_stores)
    end(three_stores)


def front_near(shards, x_in, cot, vectors, starts, kinds):
    rows = shards[1].shape[0]
    widths = [3 * shards[0].shape[2]] + [shard.shape[1] for shard in shards[1:]]
    _, length, half_width = x_in.shape
    width = 2 * half_width
    half = length // 2
    pairs = width // PAIR
    groups = [
        (widths[:1], [0, 3 * PAIR, 6 * PAIR, 9 * PAIR], G0_ORDERS),
        (widths[1:3], part_cuts(widths[1:3], *MIDDLE_CUT), REST_ORDERS),
        (widths[3:], part_cuts(widths[3:], *GATHER_CUT), REST_ORDERS),
    ]
    ff = 2 * widths[2]
    sizes = [v.shape[0] for v in vectors]
    shape = {"groups": groups, "vectors": sizes}
    dma = pltpu.SemaphoreType.DMA
    scratch = []
    for i, (_, cuts, _) in enumerate(groups):
        scratch += Gatherer.scratch_shapes(cuts, rows, i == 0)
    scratch += [
        pltpu.VMEM((length, half_width), bf16),
        pltpu.VMEM((length, half_width), bf16),
        pltpu.VMEM((length, half_width), bf16),
        pltpu.VMEM((length, width), bf16),
        pltpu.VMEM((length, width), bf16),
        pltpu.VMEM((pairs, length, 3 * PAIR), bf16),
        pltpu.VMEM((pairs, half, 6 * half), bf16),
        pltpu.VMEM((pairs, length, PAIR), f32),
        pltpu.VMEM((pairs, length, PAIR), bf16),
        pltpu.VMEM((2, half, half), f32),
        pltpu.VMEM((length, width), f32),
        pltpu.VMEM((length, width), bf16),
        pltpu.VMEM((pairs, 1, 3 * PAIR), f32),
    ]
    scratch += [dma((4,)), dma((4,)), dma((4,)), dma((4,)), dma((9,)), dma((9,)), dma((3,)), dma((4,)), dma((17,))]
    scratch += [pltpu.VMEM((size,), f32) for size in sizes]
    any_space = pl.BlockSpec(memory_space=pl.ANY)
    vmem = pl.BlockSpec(memory_space=pltpu.VMEM)
    smem = pl.BlockSpec(memory_space=pltpu.SMEM)

    def out(dims, kind=bf16):
        return jax.ShapeDtypeStruct(dims, kind)

    outs = pl.pallas_call(
        lambda *refs: front_kernel(shape, *refs),
        in_specs=[any_space] * 6 + [smem, smem] + [vmem] * 9,
        out_specs=[any_space] * 6 + [vmem] + [any_space] * 9,
        out_shape=[out((16, rows, 2 * w)) for w in widths]
        + [
            out((length, width)),
            out((length, width)),
            out((1, 2 * sum(sizes)), f32),
            out((length, 3 * width)),
            out((pairs, half, 6 * half)),
            out((length, width), f32),
            out((length, width)),
            out((length, width)),
            out((length, width), f32),
            out((length, width)),
            out((2, half, ff)),
            out((2, half, ff)),
        ],
        scratch_shapes=scratch,
        compiler_params=pltpu.CompilerParams(
            collective_id=0, has_side_effects=True, vmem_limit_bytes=67043328
        ),
        cost_estimate=pl.CostEstimate(flops=20 << 30, bytes_accessed=200 << 20, transcendentals=0),
        name="gather_weights",
    )(*shards, x_in, cot, starts, kinds, *vectors)
    full = [w.reshape(16 * rows, -1) for w in outs[:4]]
    vec = outs[6].reshape(-1)
    at = 0
    fulls = []
    for size in sizes:
        fulls.append(vec[at : at + 2 * size])
        at += 2 * size
    saved = list(outs[7:14]) + [out.reshape(length, ff) for out in outs[14:]]
    return full, list(outs[4:6]), fulls, saved


class Reducer:
    def __init__(self, place, grads, widths, cuts, scratch):
        self.z, self.y, self.core, self.x = place
        z, y, core, x = place
        self.grads = grads
        self.widths = widths
        self.acc, self.rcore = scratch[0:3], scratch[3:6]
        rx, ry, self.rz, self.cy, self.cx = scratch[6:8], scratch[8:10], scratch[10:13], scratch[13], scratch[14]
        self.final = scratch[15:18]
        (
            self.s_core, self.r_core, self.s_one, self.r_one, self.s_two, self.r_two, self.s_z, self.r_z, self.s_c,
            self.r_c, self.s_load, self.s_out,
        ) = scratch[18:]
        self.up, self.down = (row_of(z + 1, y, core), x), (row_of(z - 1, y, core), x)
        self.to_y, self.to_x = (row_of(z, 1 - y, core), x), (row_of(z, y, core), 1 - x)
        self.to_core = (row_of(z, y, 1 - core), x)
        self.by_part = [[p for p in pieces_of(widths, cuts) if p[0] == part] for part in range(3)]
        self.first = [(rx[0], self.to_x), (ry[0], self.to_y)]
        self.second = [(ry[1], self.to_y), (rx[1], self.to_x)]

    SCRATCH = 30

    @staticmethod
    def scratch_shapes(widths, cuts, rows):
        w = [cuts[i + 1] - cuts[i] for i in range(3)]
        dma = pltpu.SemaphoreType.DMA

        def low(*shape):
            return pltpu.VMEM(shape, bf16)

        scratch = [low(2, 4, 2, rows, k) for k in w] * 2
        scratch += [low(4, 2, rows, w[0]), low(4, rows, w[1])]
        scratch += [low(4, 2, rows, w[1]), low(4, rows, w[0])]
        scratch += [low(2, 4, rows, w[0]), low(2, 4, rows, w[1]), low(2, 4, 2, 2, rows, w[2])]
        scratch += [low(2, rows, w[2]), low(rows, w[2])]
        scratch += [pltpu.VMEM((rows, k), f32) for k in w]
        scratch += [dma((3,)), dma((3, 2, 4)), dma((2,)), dma((2, 4)), dma((2,)), dma((2, 4))]
        scratch += [dma((3, 2, 4)), dma((3, 2, 4)), dma((2,)), dma((2,)), dma((3,)), dma((3, 3))]
        return scratch

    def cols(self, weight, side, src, width):
        return pl.ds(pl.multiple_of(side * self.widths[weight] + src, 128), width)

    def loop(self, act):
        def step(zi, carry):
            act(zi)
            return carry

        lax.fori_loop(0, DEPTH, step, 0)

    def add(self, total, term):
        total[...] = total[...] + term[...]

    def loads(self, part):
        return [
            pltpu.make_async_copy(
                self.grads[weight].at[:, :, self.core, :, self.cols(weight, side, src, width)],
                self.acc[part].at[side, :, :, :, pl.ds(at, width)],
                self.s_load.at[part],
            )
            for i, (_, weight, at, src, width) in enumerate(self.by_part[part])
            for side in range(2)
        ]

    def view(self, part, ref, far, zi):
        if part == 0:
            return ref.at[(1 - self.x) if far else self.x, zi]
        return ref.at[:, zi, (1 - self.y) if far else self.y]

    def core_copies(self, part, far, zi):
        other = 1 - self.core
        copies = []
        for i, (_, weight, at, src, width) in enumerate(self.by_part[part]):
            cols = pl.ds(at, width)
            if part == 0:
                sides = [(1 - self.x) if far else self.x]
            else:
                sides = [0, 1]
            for k, side in enumerate(sides):
                gcols = self.cols(weight, side, src, width)
                if part == 1:
                    by = (1 - self.y) if far else self.y
                    src_ref = self.grads[weight].at[zi, by, other, :, gcols]
                    dst_ref = self.rcore[1].at[side, zi, by, :, cols]
                else:
                    src_ref = self.grads[weight].at[zi, :, other, :, gcols]
                    dst_ref = self.rcore[part].at[side, zi, :, :, cols]
                copies.append(
                    remote(
                        src_ref, dst_ref, self.s_core.at[part], self.r_core.at[part, int(far), zi], self.to_core
                    )
                )
        return copies

    def core_wait(self, part, far, zi):
        if part == 2:
            blocks = self.rcore[2].at[:, zi]
        else:
            blocks = self.view(part, self.rcore[part], far, zi)
        remote(
            blocks, blocks, self.s_core.at[part], self.r_core.at[part, int(far), zi], self.to_core
        ).wait_recv()

    def start(self, parts):
        for part in parts:
            for load in self.loads(part):
                load.start()

        def begin(far):
            def act(zi):
                for part in parts:
                    if far or part < 2:
                        for copy in self.core_copies(part, far, zi):
                            copy.start()

            self.loop(act)

        begin(True)
        begin(False)

    def first_copy(self, part, zi):
        buf, device = self.first[part]
        return remote(
            self.view(part, self.acc[part], True, zi), buf.at[zi], self.s_one.at[part], self.r_one.at[part, zi], device
        )

    def half_of(self, part, zi, far):
        if part == 0:
            return self.acc[0].at[self.x, zi, (1 - self.y) if far else self.y]
        return self.acc[1].at[(1 - self.x) if far else self.x, zi, self.y]

    def second_copy(self, part, zi):
        buf, device = self.second[part]
        return remote(self.half_of(part, zi, True), buf.at[zi], self.s_two.at[part], self.r_two.at[part, zi], device)

    def far(self, parts):
        for part in parts:
            pltpu.make_async_copy(self.rcore[part], self.acc[part], self.s_load.at[part]).wait()

        def act(zi):
            for part in parts:
                self.core_wait(part, True, zi)
                if part == 2:
                    self.add(self.acc[2].at[:, zi], self.rcore[2].at[:, zi])
                else:
                    self.add(self.view(part, self.acc[part], True, zi), self.view(part, self.rcore[part], True, zi))
                    self.first_copy(part, zi).start()

        self.loop(act)

    def near(self, parts):
        def act(zi):
            for part in parts:
                self.core_wait(part, False, zi)
                mine = self.view(part, self.acc[part], False, zi)
                self.add(mine, self.view(part, self.rcore[part], False, zi))
                self.first_copy(part, zi).wait_recv()
                self.add(mine, self.first[part][0].at[zi])
                self.second_copy(part, zi).start()

        self.loop(act)

    def last(self, parts):
        def act(zi):
            for part in parts:
                self.second_copy(part, zi).wait_recv()
                self.add(self.half_of(part, zi, False), self.second[part][0].at[zi])

        self.loop(act)

    def block(self, part, zi):
        if part == 2:
            return self.acc[2].at[:, zi]
        return self.acc[part].at[self.x, zi, self.y]

    def line_copy(self, part, direction, zd):
        return remote(
            self.block(part, zd),
            self.rz[part].at[direction, zd],
            self.s_z.at[part, direction, zd],
            self.r_z.at[part, direction, zd],
            self.down if direction else self.up,
        )

    def line(self, parts, step):
        for direction in range(2):
            at = DEPTH - 1 - step if direction else step
            for zd in (0, 1, 2) if direction else (3, 2, 1):
                if not ((at > zd) if direction else (at < zd)):
                    continue
                for part in parts:

                    def act(part=part, direction=direction, zd=zd):
                        if step > 0:
                            self.line_copy(part, direction, zd).wait_recv()
                            self.add(self.block(part, zd), self.rz[part].at[direction, zd])
                        self.line_copy(part, direction, zd).start()

                    pl.when(self.z == at)(act)

    def line_end(self, parts):
        for part in parts:
            for direction in range(2):

                def act(part=part, direction=direction):
                    self.line_copy(part, direction, self.z).wait_recv()
                    self.add(self.block(part, self.z), self.rz[part].at[direction, self.z])

                pl.when((self.z < DEPTH - 1) if direction else (self.z > 0))(act)

    def y_copy(self):
        return remote(self.acc[2].at[:, self.z, 1 - self.y], self.cy, self.s_c.at[0], self.r_c.at[0], self.to_y)

    def x_copy(self):
        return remote(self.acc[2].at[1 - self.x, self.z, self.y], self.cx, self.s_c.at[1], self.r_c.at[1], self.to_x)

    def turn(self):
        self.y_copy().wait_recv()
        self.add(self.acc[2].at[:, self.z, self.y], self.cy)
        self.x_copy().start()

    def turn_end(self):
        self.x_copy().wait_recv()
        self.add(self.acc[2].at[self.x, self.z, self.y], self.cx)

    def stores(self, outs):
        if len(outs[0].shape) == 3:
            return [
                pltpu.make_async_copy(
                    self.final[part].at[:, pl.ds(which * PAIR, PAIR)],
                    outs[0].at[which, :, pl.ds(part * PAIR, PAIR)],
                    self.s_out.at[part, which],
                )
                for part in range(3)
                for which in range(3)
            ]
        return [
            pltpu.make_async_copy(
                self.final[part].at[:, pl.ds(at, width)], outs[weight].at[:, pl.ds(src, width)], self.s_out.at[part, i]
            )
            for part in range(3)
            for i, (_, weight, at, src, width) in enumerate(self.by_part[part])
        ]

    def finish(self, outs):
        for part in range(3):
            self.final[part][...] = self.acc[part][self.x, self.z, self.y].astype(f32)
        for store in self.stores(outs):
            store.start()

    def drain(self, outs):
        for part in range(3):
            remote(
                self.acc[part], self.rcore[part], self.s_core.at[part], self.r_core.at[part, 0, 0], self.to_core
            ).wait_send()
            for direction in range(2):
                for zd in range(DEPTH):
                    pl.when((self.z > zd) if direction else (self.z < zd))(
                        lambda part=part, direction=direction, zd=zd: self.line_copy(part, direction, zd).wait_send()
                    )
            if part < 2:
                for (buf, device), send, recv in (
                    (self.first[part], self.s_one, self.r_one),
                    (self.second[part], self.s_two, self.r_two),
                ):
                    remote(buf, buf, send.at[part], recv.at[part, 0], device).wait_send()
        self.y_copy().wait_send()
        self.x_copy().wait_send()
        for store in self.stores(outs):
            store.wait()


def back_kernel(shape, *refs):
    (
        g_out, g_fc, g_proj, packed, attended, p_all, inv_all, gatt, normed_t, w_qkv, x_all, middle, gain_ref, small_in,
        o_qkv, o_out, o_fc, o_proj, o_sum, o_input,
    ) = refs[:20]
    scr = refs[20:]
    first = Reducer.SCRATCH
    place = my_place()
    z, y, core, x = place
    early = Reducer(place, [g_out, g_fc, g_proj], shape["early"], shape["early_cuts"], scr[:first])
    qkv, o_buf, p_buf, inv_buf, g_buf, nt_buf, w_buf, x_buf, m_buf, gqkv, gi, col_sum, srecv, sacc, sums = scr[2 * first : 2 * first + 15]
    s_all, s_pair, s_mid, s_gi, r_gi, l_gi, s_s, r_s = scr[2 * first + 15 :]
    late = Reducer(place, [gqkv], shape["late"], shape["late_cuts"], scr[first : 2 * first])
    whole = [
        pltpu.make_async_copy(packed, qkv, s_all.at[0]),
        pltpu.make_async_copy(normed_t, nt_buf, s_all.at[1]),
        pltpu.make_async_copy(w_qkv, w_buf, s_all.at[2]),
        pltpu.make_async_copy(x_all, x_buf, s_all.at[3]),
    ]

    def pair_loads(step):
        j = (step // 2 + 2) % 3 + 3 * (step % 2)
        slot = step % 2
        cols = pl.ds(pl.multiple_of(j * PAIR, PAIR), PAIR)
        return [
            pltpu.make_async_copy(p_all.at[j], p_buf.at[slot], s_pair.at[slot, 0]),
            pltpu.make_async_copy(attended.at[:, cols], o_buf.at[slot], s_pair.at[slot, 1]),
            pltpu.make_async_copy(inv_all.at[:, cols], inv_buf.at[slot], s_pair.at[slot, 2]),
            pltpu.make_async_copy(gatt.at[:, cols], g_buf.at[slot], s_pair.at[slot, 3]),
        ]

    begin(whole[:1])
    begin(pair_loads(0))
    begin(whole[1:])
    to_z1 = (row_of(z + 1 - 2 * (z % 2), y, core), x)
    to_z2 = (row_of((z + 2) % 4, y, core), x)
    greet([early.to_core, early.to_x, early.to_y, to_z2], z, early.up, early.down)
    early.start((0, 1, 2))
    end(whole[:1])

    def pair(step, carry):
        j = (step // 2 + 2) % 3 + 3 * (step % 2)
        slot = step % 2
        pl.when(step < 5)(lambda: begin(pair_loads(step + 1)))
        end(pair_loads(step))
        cols = pl.ds(pl.multiple_of(3 * PAIR * j, PAIR), 3 * PAIR)
        attend_back_pair(qkv.at[:, cols], o_buf.at[slot], p_buf.at[slot], inv_buf.at[slot], g_buf.at[slot], col_sum.at[j])
        pl.when(step == 0)(lambda: end(whole[1:2]))
        grad = nn(nt_buf[...], qkv[:, cols]).astype(bf16)
        gqkv[:, :, :, :, cols] = grad.reshape(gqkv.shape[:4] + (3 * PAIR,))
        for k, serve in enumerate(serves):
            pl.when(step == k)(serve)
        return carry

    rows = m_buf.shape[1]
    blocks = x_buf.shape[0] // rows

    def mid_load(i):
        return pltpu.make_async_copy(middle.at[pl.ds(pl.multiple_of(i * rows, rows), rows)], m_buf.at[i % 2], s_mid.at[i % 2])

    def input_copies(i):
        span = pl.ds(pl.multiple_of(i * rows, rows), rows)
        return (
            pltpu.make_async_copy(gi.at[0, span], o_input.at[x, span], l_gi.at[i]),
            remote(gi.at[1, span], o_input.at[x, span], s_gi.at[i], r_gi.at[i], early.to_x),
        )

    def input_block(i):
        span = pl.ds(pl.multiple_of(i * rows, rows), rows)
        grad = nt(qkv[span, :], w_buf[...])
        pl.when(i + 1 < blocks)(lambda: mid_load(i + 1).start())
        mid_load(i).wait()
        value = x_buf[span, :].astype(f32)
        width = value.shape[1]
        average = jnp.sum(value, axis=1, keepdims=True) / width
        square = jnp.sum(value * value, axis=1, keepdims=True) / width
        inverse = lax.rsqrt(square - average * average + epsilon)
        centred = (value - average) * inverse
        scaled = grad * gain_ref[...]
        one = jnp.sum(scaled, axis=1, keepdims=True) / width
        two = jnp.sum(scaled * centred, axis=1, keepdims=True) / width
        out = m_buf[i % 2] + inverse * (scaled - one - centred * two)
        for k, term in enumerate((grad * centred, grad)):
            sums[k] = sums[k] + jnp.sum(term, axis=0, keepdims=True)
        half = width // 2
        is_low = x == 0
        gi[0, span, :] = jnp.where(is_low, out[:, :half], out[:, half:]).astype(bf16)
        gi[1, span, :] = jnp.where(is_low, out[:, half:], out[:, :half]).astype(bf16)
        for copy in input_copies(i):
            copy.start()

    partners = [early.to_core, early.to_x, early.to_y, to_z1, to_z2]

    def small_copy(step):
        return remote(sacc.at[step], srecv.at[step], s_s.at[step], r_s.at[step], partners[step])

    def small_start():
        sacc[0] = small_in[...]
        at = 0
        for k in range(2):
            for i in range(6):
                sacc[0, at : at + 1, :] = sums[k][:, i * PAIR : (i + 1) * PAIR]
                at += 1
        for k in range(2):
            for i in range(6):
                sacc[0, at : at + 1, :] = col_sum[i, k]
                at += 1
        small_copy(0).start()

    def small_next(step):
        small_copy(step).wait()
        sacc[step + 1] = sacc[step] + srecv[step]
        if step < 4:
            small_copy(step + 1).start()

    both = (0, 1)

    def serve_0():
        early.far((0, 1, 2))
        early.line((2,), 0)

    def serve_1():
        late.start((2,))

    def serve_2():
        early.line((2,), 1)

    def serve_3():
        late.start((0,))
        late.far((2,))
        early.line((2,), 2)
        late.line((2,), 0)
        mid_load(0).start()

    def serve_4():
        early.near(both)
        late.far((0,))

    def serve_5():
        late.start((1,))
        early.line_end((2,))
        early.y_copy().start()
        late.line((2,), 1)
        end(whole[2:])

    serves = (serve_0, serve_1, serve_2, serve_3, serve_4, serve_5)
    lax.fori_loop(0, 6, pair, 0)

    def block_0():
        early.last(both)
        early.line(both, 0)
        late.far((1,))
        late.line((2,), 2)

    def block_1():
        early.turn()
        early.line(both, 1)
        late.near((0,))
        late.line_end((2,))
        late.y_copy().start()

    def block_2():
        early.turn_end()
        early.line(both, 2)
        late.near((1,))
        late.turn()

    after = (block_0, block_1, block_2)
    sums[...] = jnp.zeros(sums.shape, f32)

    def input_step(i, carry):
        input_block(i)
        for k, serve in enumerate(after):
            pl.when(i == k)(serve)
        return carry

    lax.fori_loop(0, blocks, input_step, 0)
    small_start()
    late.last((0,))
    late.line((0,), 0)
    early.line_end(both)
    early.finish([o_out, o_fc, o_proj])
    small_next(0)
    late.last((1,))
    late.line((1,), 0)
    late.turn_end()
    late.line(both, 1)
    small_next(1)
    late.line(both, 2)
    small_next(2)
    late.line_end(both)
    late.finish([o_qkv])
    small_next(3)
    small_next(4)
    o_sum[...] = sacc[5]
    for i in range(blocks):
        local, other = input_copies(i)
        local.wait()
        other.wait()
    early.drain([o_out, o_fc, o_proj])
    late.drain([o_qkv])


def back_near(grads, packed, attended, p, inv, gatt, normed_t, w_qkv, x, middle, gain, small, rows):
    length, width = x.shape
    wide = packed.shape[1]
    early = [grad.shape[1] // 2 for grad in grads]
    shape = {"early": early, "early_cuts": part_cuts(early, *REDUCE_CUT), "late": [wide // 2]}
    shape["late_cuts"] = [0, wide // 6, wide // 3, wide // 2]
    dma = pltpu.SemaphoreType.DMA
    half = length // 2
    blocks = 4
    scratch = Reducer.scratch_shapes(early, shape["early_cuts"], rows)
    scratch += Reducer.scratch_shapes(shape["late"], shape["late_cuts"], rows)
    scratch += [
        pltpu.VMEM((length, wide), bf16),
        pltpu.VMEM((2, length, PAIR), bf16),
        pltpu.VMEM((2, half, 6 * half), bf16),
        pltpu.VMEM((2, length, PAIR), f32),
        pltpu.VMEM((2, length, PAIR), bf16),
        pltpu.VMEM((width, length), bf16),
        pltpu.VMEM((width, wide), bf16),
        pltpu.VMEM((length, width), bf16),
        pltpu.VMEM((2, length // blocks, width), f32),
        pltpu.VMEM((4, 2, 2, rows, wide), bf16),
        pltpu.VMEM((2, length, width // 2), bf16),
        pltpu.VMEM((width // PAIR, 2, 1, PAIR), f32),
        pltpu.VMEM((5,) + small.shape, f32),
        pltpu.VMEM((6,) + small.shape, f32),
        pltpu.VMEM((2, 1, width), f32),
    ]
    scratch += [dma((4,)), dma((2, 4)), dma((2,)), dma((4,)), dma((4,)), dma((4,)), dma((5,)), dma((5,))]
    shaped = [grad.reshape(4, 2, 2, rows, grad.shape[1]) for grad in grads]
    any_space = pl.BlockSpec(memory_space=pl.ANY)
    vmem = pl.BlockSpec(memory_space=pltpu.VMEM)
    outs = pl.pallas_call(
        lambda *refs: back_kernel(shape, *refs),
        in_specs=[any_space] * 12 + [vmem, vmem],
        out_specs=[any_space] * 4 + [vmem, any_space],
        out_shape=[jax.ShapeDtypeStruct((3, rows, wide // 6), f32)]
        + [jax.ShapeDtypeStruct((rows, w), f32) for w in early]
        + [jax.ShapeDtypeStruct(small.shape, f32), jax.ShapeDtypeStruct((2, length, width // 2), bf16)],
        scratch_shapes=scratch,
        compiler_params=pltpu.CompilerParams(
            collective_id=1, has_side_effects=True, vmem_limit_bytes=67043328
        ),
        cost_estimate=pl.CostEstimate(flops=30 << 30, bytes_accessed=200 << 20, transcendentals=0),
        name="reduce_grads",
    )(*shaped, packed, attended, p, inv, gatt, normed_t, w_qkv, x, middle, gain.reshape(1, -1), small)
    return outs


def gather_far(shards):
    fulls = []
    for shard in shards:
        rows = lax.all_gather(shard, ("col", "row"), axis=0, tiled=True)
        fulls.append(jnp.concatenate(jnp.split(rows, 2, axis=0), axis=1))
    return fulls


def reduce_far(grads, small):
    outs = []
    for grad in grads:
        halves = jnp.concatenate(jnp.split(grad, 2, axis=1), axis=0)
        outs.append(lax.psum_scatter(halves, ("col", "row"), scatter_dimension=0, tiled=True).astype(f32))
    return outs, lax.psum(small, ("row", "col"))


def part_cuts(widths, first, second):
    total = sum(widths) // 128
    one = round(total * first)
    two = round(total * (first + second))
    return [0, one * 128, two * 128, total * 128]


def layer_norm(value):
    width = value.shape[-1]
    average = jnp.sum(value, axis=-1, keepdims=True) / width
    square = jnp.sum(value * value, axis=-1, keepdims=True) / width
    inverse = lax.rsqrt(square - average * average + epsilon)
    return (value - average) * inverse, inverse


def norm_backward(grad, centred, inverse, gain):
    scaled = grad * gain
    first = jnp.mean(scaled, axis=-1, keepdims=True)
    second = jnp.mean(scaled * centred, axis=-1, keepdims=True)
    back = inverse * (scaled - first - centred * second)
    return back, jnp.sum(grad * centred, axis=0), jnp.sum(grad, axis=0)


def by_pairs(block):
    rows, three, half = block.shape
    return block.reshape(rows, three, half // PAIR, PAIR).transpose(0, 2, 1, 3).reshape(rows, three * half)


def body(
    near, x_in, span_start, span_kind, ln1_gain, ln1_bias, w_qkv, b_query, b_value, w_out, b_out,
    ln2_gain, ln2_bias, w_fc, b_fc, w_proj, b_proj, cotangent,
):
    half_width = x_in.shape[2]
    shard = w_qkv.shape[0]
    col = lax.axis_index("col")

    vectors = [ln1_gain, ln1_bias, b_query, b_value, b_out, ln2_gain, ln2_bias, b_fc, b_proj]
    shards = [w_out.T, w_fc, w_proj.T]
    width = 2 * half_width
    if near:
        weights, (x_own, grad_out), vectors, saved = front_near(
            [w_qkv.transpose(1, 0, 2)] + shards, x_in, cotangent, vectors, span_start, span_kind
        )
        qkv_all, out_all, fc_all, proj_all = weights
        ln1_gain, _, _, _, _, ln2_gain, _, _, b_proj = vectors
        packed, p, inv, attended, normed_first, middle, normed_second, active, slope = saved
        centred_second, inverse_second = layer_norm(middle)
    else:
        x_own = own_micro(x_in)
        residual = x_own.astype(f32)
        grad_out = own_micro(cotangent)
        qkv_all, out_all, fc_all, proj_all = gather_far([by_pairs(w_qkv)] + shards)
        flat = jnp.concatenate(vectors)
        flat_other = swap(flat)
        full = []
        at = 0
        for vector in vectors:
            full.append(ordered(vector, flat_other[at : at + vector.shape[0]], 0))
            at += vector.shape[0]
        ln1_gain, ln1_bias, b_query, b_value, b_out, ln2_gain, ln2_bias, b_fc, b_proj = full
        starts = lax.dynamic_index_in_dim(span_start, col, 0, keepdims=False)[0]
        kinds = lax.dynamic_index_in_dim(span_kind, col, 0, keepdims=False)[0]
        spans = jnp.stack([starts, kinds])
        centred_first, inverse_first = layer_norm(residual)
        normed_first = (centred_first * ln1_gain + ln1_bias).astype(bf16)
        bias = jnp.stack([b_query, jnp.zeros_like(b_query), b_value]).reshape(3, -1, PAIR)
        packed = (nn(normed_first, qkv_all) + bias.transpose(1, 0, 2).reshape(-1)).astype(bf16)
        attended, p, inv = attend_forward(packed, spans)
        middle = residual + nt(attended, out_all) + b_out
        centred_second, inverse_second = layer_norm(middle)
        normed_second = (centred_second * ln2_gain + ln2_bias).astype(bf16)
        hidden = nn(normed_second, fc_all) + b_fc
        squared = hidden * hidden
        tanh = jnp.tanh(GELU_A * hidden * (1.0 + GELU_B * squared))
        active = (0.5 * hidden * (1.0 + tanh)).astype(bf16)
        slope = (
            0.5 * (1.0 + tanh)
            + 0.5 * hidden * (1.0 - tanh * tanh) * GELU_A * (1.0 + 3.0 * GELU_B * squared)
        ).astype(bf16)
    layer_out = back_micro((middle + nt(active, proj_all) + b_proj).astype(bf16))

    grad_out_wide = grad_out.astype(f32)
    g_proj = tn(grad_out, active).astype(bf16)
    grad_hidden = (nn(grad_out, proj_all) * slope.astype(f32)).astype(bf16)
    g_fc = tn(normed_second, grad_hidden).astype(bf16)
    g_bfc = jnp.sum(grad_hidden.astype(f32), axis=0)
    grad_normed = nt(grad_hidden, fc_all)
    back, g_ln2_gain, g_ln2_bias = norm_backward(grad_normed, centred_second, inverse_second, ln2_gain)
    grad_middle = grad_out_wide + back
    g_bproj = jnp.sum(grad_out_wide, axis=0)
    g_bout = jnp.sum(grad_middle, axis=0)
    grad_low = grad_middle.astype(bf16)
    g_out = tn(grad_low, attended).astype(bf16)
    grad_attended = nn(grad_low, out_all).astype(bf16)
    zeros = jnp.zeros((width,), f32)
    small = [zeros, zeros, zeros, zeros, g_bout, g_ln2_gain, g_ln2_bias, g_bfc, g_bproj]
    if near:
        flat = jnp.concatenate(small).reshape(-1, 128)
        *outs, summed, grad_input = back_near(
            [g_out, g_fc, g_proj], packed, attended, p, inv, grad_attended, normed_first.T, qkv_all,
            x_own, grad_middle, ln1_gain, flat, shard,
        )
        outs[0] = outs[0].transpose(1, 0, 2)
    else:
        grad_packed, sums = attend_backward(packed, attended, p, inv, grad_attended)
        g_qkv = tn(normed_first, grad_packed).astype(bf16)
        grad_normed = nt(grad_packed, qkv_all)
        back, g_ln1_gain, g_ln1_bias = norm_backward(grad_normed, centred_first, inverse_first, ln1_gain)
        grad_input = back_micro((grad_middle + back).astype(bf16))
        small[:4] = [g_ln1_gain, g_ln1_bias, sums[:, 0, 0].reshape(-1), sums[:, 1, 0].reshape(-1)]
        outs, summed = reduce_far([g_qkv, g_out, g_fc, g_proj], jnp.concatenate(small))
        outs[0] = outs[0].reshape(shard, -1, 3, PAIR).transpose(0, 2, 1, 3).reshape(shard, 3, half_width)
    out_qkv, out_out, out_fc, out_proj = outs
    summed = summed.reshape(-1)
    kept = []
    at = 0
    for vector in small:
        size = vector.shape[0] // 2
        kept.append(lax.dynamic_slice_in_dim(summed, at + col * size, size, 0))
        at += vector.shape[0]
    return (
        layer_out,
        grad_input,
        kept[0],
        kept[1],
        out_qkv,
        kept[2],
        kept[3],
        out_out.T,
        kept[4],
        kept[5],
        kept[6],
        out_fc,
        kept[7],
        out_proj.T,
        kept[8],
    )


def solution(mesh):
    placed = (
        P(None, "row", "col"), P(None, "row", None), P(None, "row", None), P("col"), P("col"),
        P("row", None, "col"), P("col"), P("col"), P("col", "row"), P("col"), P("col"), P("col"),
        P("row", "col"), P("col"), P("col", "row"), P("col"), P(None, "row", "col"),
    )
    near = mesh.shape["row"] == 16
    return jax.shard_map(
        partial(body, near),
        mesh=mesh,
        in_specs=placed,
        out_specs=(
            P(None, "row", "col"), P(None, "row", "col"), P("col"), P("col"), P("row", None, "col"),
            P("col"), P("col"), P("col", "row"), P("col"), P("col"), P("col"), P("row", "col"),
            P("col"), P("col", "row"), P("col"),
        ),
        check_vma=False,
    )
```

profile of v0, /device:TPU:0, one launch (start us, length us, event | category | flops | bytes accessed | tf_op | source)
XLA Modules:
  0.0 246.4 jit_solution(2063657033942210611)
XLA Ops:
  0.7 95.2 %gather_weights.1 = (bf16[16,48,2304]{2,1,0:T(8,128)(2,1)}, bf16[16,48,768]{2,1,0:T(8,128)(2,1)}, bf16[16,48,3072]{2,1,0:T(8,128)(2,1)}, bf16[16,48,3072]{2,1,0:...) custom-call(bf16[3,48,384]{2,1,0:T(8,128)(2,1)} %bitcast.43, ...), custom_call_target="tpu_custom_call" | custom-call | flops 21474836480 | bytes 209715200 | tf_op jit(solution)/shard_map/gather_weights/pallas_call | solution.py:722
  95.9 1.3 slice_reduce_fusion
  97.2 10.3 %add_convert_fusion = bf16[1024,768]{1,0:T(8,128)(2,1)S(1)} fusion(f32[1024,768]{1,0:T(8,128)} %get-tuple-element.37, bf16[1024,3072]{1,0:T(8,128)(2,1)} %bitcast.48, bf16[768,3072]{1,0:T(8,128)(2,1)} %bitcast.56, f32[768]{0:T(1024)S(1)} %get-tuple-element.66), kind=kOutput, calls=%fused_computation.11 | convolution fusion | flops 4834197504 | bytes 15731712 | tf_op jit(solution)/shard_map/dot_general | solution.py:25
  107.6 1.0 constant_dynamic-slice_fusion
  108.6 1.0 collective-permute-start
  110.1 6.9 %convolution_convert_fusion = bf16[768,3072]{1,0:T(8,128)(2,1)} fusion(bf16[1024,768]{1,0:T(8,128)(2,1)S(1)} %copy-done.5, bf16[1024,3072]{1,0:T(8,128)(2,1)S(1)} %bitcast.51), kind=kOutput, calls=%fused_computation.3 | convolution fusion | flops 4834197504 | bytes 12582912 | tf_op jit(solution)/shard_map/dot_general | solution.py:29
  117.0 7.1 %convert_reduce_fusion = (f32[3072]{0:T(1024)S(1)}, bf16[1024,3072]{1,0:T(8,128)(2,1)}) fusion(bf16[1024,3072]{1,0:T(8,128)(2,1)S(1)} %bitcast.47, bf16[1024,768]{1,0:T(8,128)(2,1)S(1)} %copy-done.5, bf16[768,3072]{1,0:T(8,128)(2,1)S(1)} %bitcast.59), kind=kOutput, calls=%fused_computation.2 | convolution fusion | flops 4847563776 | bytes 18886656 | tf_op jit(solution)/shard_map/dot_general | solution.py:21
  124.1 7.9 %multiply_reduce_fusion = (f32[768]{0:T(1024)S(1)}, f32[1024]{0:T(1024)S(1)}, f32[1024]{0:T(1024)S(1)}, f32[768]{0:T(1024)S(1)}, f32[1024,768]{1,0:T(8,128)S(1)}) fusion(f32[1024,768]{1,0:T(8,128)S(1)} %copy-done, f32[1024]{0:T(1024)S(1)} %get-tuple-element.82, f32[1024]{0:T(1024)S(1)} %get-tuple-element.81, f32[768]{0:T(1024)S(1)} %get-tuple-element.65, ...), kind=kOutput, calls=%fused_computation.7 | convolution fusion | flops 4838912000 | bytes 17327104 | tf_op jit(solution)/shard_map/dot_general | solution.py:25
  132.1 1.6 fusion.3
  133.7 2.6 %convolution_convert_fusion.2.refs_7_ = bf16[1024,768]{1,0:T(8,128)(2,1)} fusion(bf16[768,768]{1,0:T(8,128)(2,1)S(1)} %bitcast.62, f32[1024,768]{1,0:T(8,128)S(1)} %get-tuple-element.68.refs_11_), kind=kOutput, calls=%fused_computation.13 | convolution fusion | flops 1209532416 | bytes 5898240 | tf_op jit(solution)/shard_map/dot_general | solution.py:21
  136.3 2.5 %convolution_convert_fusion.3 = bf16[768,768]{1,0:T(8,128)(2,1)} fusion(bf16[1024,768]{1,0:T(8,128)(2,1)S(1)} %copy-done.12, f32[1024,768]{1,0:T(8,128)S(1)} %get-tuple-element.68.refs_11_), kind=kOutput, calls=%fused_computation.15 | convolution fusion | flops 1209335808 | bytes 5898240 | tf_op jit(solution)/shard_map/dot_general | solution.py:29
  138.8 7.2 %convolution_convert_fusion.1 = bf16[768,3072]{1,0:T(8,128)(2,1)} fusion(bf16[1024,768]{1,0:T(8,128)(2,1)S(1)} %copy-done.13, bf16[1024,3072]{1,0:T(8,128)(2,1)S(1)} %bitcast.65), kind=kOutput, calls=%fused_computation.4 | convolution fusion | flops 4834197504 | bytes 12582912 | tf_op jit(solution)/shard_map/dot_general | solution.py:29
  146.0 1.6 copy.32
  147.7 0.6 copy-done.10
  148.3 87.7 %reduce_grads.1 = (f32[3,48,384]{2,1,0:T(8,128)}, f32[48,384]{1,0:T(8,128)}, f32[48,1536]{1,0:T(8,128)}, f32[48,1536]{1,0:T(8,128)}, f32[72,128]{1,0:T(8,128)}, /*index=5*/bf16[2,1024,384]{2,1,0:T(8,128)(2,1)}) custom-call(bf16[4,2,2,48,768]{4,3,2,1,0:T(8,128)(2,1)} %bitcast.63, bf16[4,2,2,48,3072]{4,3,2,1,0:T(8,128)(2,1)} %bitcast.60, ...), custom_call_target="tpu_custom_call" | custom-call | flops 32212254720 | bytes 209715200 | tf_op jit(solution)/shard_map/reduce_grads/pallas_call | solution.py:1266
  236.0 1.4 dynamic_slice.42
  237.4 1.5 fusion.4
  238.9 1.8 select_bitcast_fusion.1
  240.7 1.3 pad_maximum_fusion
  242.1 1.1 copy.43
  243.2 0.7 copy.44
  243.9 0.6 copy.45
  244.5 0.7 copy.46
  245.2 0.7 copy.47
  (62 shorter events, 0.6 us)
Async XLA Ops:
  97.2 12.8 %slice-start.2 = ((s8[6291456]{0:T(1024)(128)(4,1)}), s8[4194304]{0:T(1024)(128)(4,1)S(1)}, s32[]{:S(2)}) async-start(s8[6291456]{0:T(1024)(128)(4,1)} %bitcast.49), calls=%async_computation.2 | async-start | bytes 8388608
  97.2 12.4 %copy-start = (f32[1024,768]{1,0:T(8,128)S(1)}, f32[1024,768]{1,0:T(8,128)}, u32[]{:S(2)}) copy-start(f32[1024,768]{1,0:T(8,128)} %get-tuple-element.37) | copy-start | bytes 9437188
  97.2 12.8 %slice-start.3 = ((s8[6291456]{0:T(1024)(128)(4,1)}), s8[2097152]{0:T(1024)(128)(4,1)S(1)}, s32[]{:S(2)}) async-start(s8[6291456]{0:T(1024)(128)(4,1)} %bitcast.49), calls=%async_computation.3 | async-start | bytes 4194304
  107.6 9.4 %copy-start.4 = (bf16[1024,768]{1,0:T(8,128)(2,1)}, bf16[1024,768]{1,0:T(8,128)(2,1)S(1)}, u32[]{:S(2)}) copy-start(bf16[1024,768]{1,0:T(8,128)(2,1)S(1)} %add_convert_fusion) | copy-start | bytes 4718596
  107.6 2.5 copy-start.5
  108.6 130.3 %collective-permute-start = (bf16[1024,384]{1,0:T(8,128)(2,1)}, bf16[1024,384]{1,0:T(8,128)(2,1)}, u32[]{:S(2)}, u32[]{:S(2)}) collective-permute-start(bf16[1024,384]{1,0:T(8,128)(2,1)} %constant_dynamic-slice_fusion), channel_id=1, source_target_pairs={{0,1},{1,0},{2,3},{3,2},{4,5},{5,4},{6,7},{7,6},{8,9},{9,8},{10,11... | collective-permute-start | bytes 2359304 | tf_op jit(solution)/shard_map/ppermute | solution.py:203
  109.6 7.4 %slice-start = ((s8[6291456]{0:T(1024)(128)(4,1)}), s8[4194304]{0:T(1024)(128)(4,1)S(1)}, s32[]{:S(2)}) async-start(s8[6291456]{0:T(1024)(128)(4,1)} %bitcast.45), calls=%async_computation | async-start | bytes 8388608
  109.6 7.4 %slice-start.6 = ((s8[4718592]{0:T(1024)(128)(4,1)}), s8[4194304]{0:T(1024)(128)(4,1)S(1)}, s32[]{:S(2)}) async-start(s8[4718592]{0:T(1024)(128)(4,1)} %bitcast.57), calls=%async_computation.6 | async-start | bytes 8388608
  110.0 7.0 %slice-start.1 = ((s8[6291456]{0:T(1024)(128)(4,1)}), s8[2097152]{0:T(1024)(128)(4,1)S(1)}, s32[]{:S(2)}) async-start(s8[6291456]{0:T(1024)(128)(4,1)} %bitcast.45), calls=%async_computation.1 | async-start | bytes 4194304
  110.0 7.0 %slice-start.7 = ((s8[4718592]{0:T(1024)(128)(4,1)}), s8[524288]{0:T(1024)(128)(4,1)S(1)}, s32[]{:S(2)}) async-start(s8[4718592]{0:T(1024)(128)(4,1)} %bitcast.57), calls=%async_computation.7 | async-start | bytes 1048576
  110.1 14.1 %slice-start.4 = ((s8[4718592]{0:T(1024)(128)(4,1)}), s8[524288]{0:T(1024)(128)(4,1)S(1)}, s32[]{:S(2)}) async-start(s8[4718592]{0:T(1024)(128)(4,1)} %bitcast.53), calls=%async_computation.4 | async-start | bytes 1048576
  117.0 7.1 %slice-start.5 = ((s8[4718592]{0:T(1024)(128)(4,1)}), s8[4194304]{0:T(1024)(128)(4,1)S(1)}, s32[]{:S(2)}) async-start(s8[4718592]{0:T(1024)(128)(4,1)} %bitcast.53), calls=%async_computation.5 | async-start | bytes 8388608
  132.1 1.6 copy-start.11
  132.1 6.7 %slice-start.8 = ((s8[6291456]{0:T(1024)(128)(4,1)}), s8[4194304]{0:T(1024)(128)(4,1)S(1)}, s32[]{:S(2)}) async-start(s8[6291456]{0:T(1024)(128)(4,1)} %bitcast.64), calls=%async_computation.8 | async-start | bytes 8388608
  133.7 2.6 %copy-start.1 = (f32[1024,768]{1,0:T(8,128)}, f32[1024,768]{1,0:T(8,128)S(1)}, u32[]{:S(2)}) copy-start(f32[1024,768]{1,0:T(8,128)S(1)} %get-tuple-element.68.refs_11_) | copy-start | bytes 9437188
  133.7 2.6 %copy-start.12 = (bf16[1024,768]{1,0:T(8,128)(2,1)S(1)}, bf16[1024,768]{1,0:T(8,128)(2,1)}, u32[]{:S(2)}) copy-start(bf16[1024,768]{1,0:T(8,128)(2,1)} %get-tuple-element.44.refs_4_) | copy-start | bytes 4718596
  133.7 5.1 %slice-start.9 = ((s8[6291456]{0:T(1024)(128)(4,1)}), s8[2097152]{0:T(1024)(128)(4,1)S(1)}, s32[]{:S(2)}) async-start(s8[6291456]{0:T(1024)(128)(4,1)} %bitcast.64), calls=%async_computation.9 | async-start | bytes 4194304
  136.3 2.5 %copy-start.13 = (bf16[1024,768]{1,0:T(8,128)(2,1)S(1)}, bf16[1024,768]{1,0:T(8,128)(2,1)}, u32[]{:S(2)}) copy-start(bf16[1024,768]{1,0:T(8,128)(2,1)} %get-tuple-element.45) | copy-start | bytes 4718596
  138.8 7.2 %copy-start.3 = (bf16[1024,768]{1,0:T(8,128)(2,1)S(1)}, bf16[1024,768]{1,0:T(8,128)(2,1)}, u32[]{:S(2)}) copy-start(bf16[1024,768]{1,0:T(8,128)(2,1)} %get-tuple-element.50) | copy-start | bytes 4718596
  238.9 3.2 %copy-start.2 = (bf16[2,1024,384]{2,1,0:T(8,128)(2,1)S(1)}, bf16[2,1024,384]{2,1,0:T(8,128)(2,1)}, u32[]{:S(2)}) copy-start(bf16[2,1024,384]{2,1,0:T(8,128)(2,1)} %get-tuple-element.104) | copy-start | bytes 4718596
  240.7 2.5 %copy-start.8 = (f32[3,48,384]{2,1,0:T(8,128)S(1)}, f32[3,48,384]{2,1,0:T(8,128)}, u32[]{:S(2)}) copy-start(f32[3,48,384]{2,1,0:T(8,128)} %get-tuple-element.55) | copy-start | bytes 663556
  240.7 3.2 %copy-start.9 = (f32[48,384]{1,0:T(8,128)S(1)}, f32[48,384]{1,0:T(8,128)}, u32[]{:S(2)}) copy-start(f32[48,384]{1,0:T(8,128)} %get-tuple-element.56) | copy-start | bytes 221188
  240.7 3.8 %copy-start.7 = (f32[48,1536]{1,0:T(8,128)S(1)}, f32[48,1536]{1,0:T(8,128)}, u32[]{:S(2)}) copy-start(f32[48,1536]{1,0:T(8,128)} %get-tuple-element.114) | copy-start | bytes 884740
  240.7 4.5 %copy-start.6 = (f32[48,1536]{1,0:T(8,128)S(1)}, f32[48,1536]{1,0:T(8,128)}, u32[]{:S(2)}) copy-start(f32[48,1536]{1,0:T(8,128)} %get-tuple-element.58) | copy-start | bytes 884740
  (1 other events, 0.6 us)
where the time goes:
time: 250 us; the launch traced here: 246 us
  Pallas kernels  183 us (73%)
  matrix products  44.5 us (18%)
  local copies, waits for them, and re-layouts  11.4 us (5%)
  other arithmetic  5.14 us (2%)
    pallas_call x1, Pallas kernels, front_near(): pl.pallas_call(lambda *refs: front_kernel(shape, *refs), in_specs=[any_sp...  95.2 us
    pallas_call x1, Pallas kernels, back_near(): pl.pallas_call(lambda *refs: back_kernel(shape, *refs), in_specs=[any_spa...  87.7 us
    dot_general x2, matrix products, nt(): lax.dot_general(a, b, (((1,), (1,)), ((), ())), preferred_element_type=f32)  18.2 us
    dot_general x3, matrix products, tn(): lax.dot_general(a, b, (((0,), (0,)), ((), ())), preferred_element_type=f32)  16.6 us
    dot_general x2, matrix products, nn(): lax.dot_general(a, b, (((1,), (0,)), ((), ())), preferred_element_type=f32)  9.63 us
  transfers between devices with their start and end apart: 1, of which 0 were waited for; matrix products, arithmetic and copies ran while one was open for 17% of the time, Pallas kernels for 36%

commit v1 on v0

--- a/solution.py
+++ b/solution.py
@@ -227,9 +227,10 @@
 
 
 G0_ORDERS = ("xzy", "xzy", "xyz")
-REST_ORDERS = ("zxy", "zxy", "xyz")
-MIDDLE_CUT = (5 / 15, 6 / 15)
-GATHER_CUT = (4 / 12, 4 / 12)
+MIDDLE_ORDERS = ("zxy", "xyz")
+REST_ORDERS = ("zxy", "xyz")
+MIDDLE_CUT = (11 / 15,)
+GATHER_CUT = (9 / 12,)
 REDUCE_CUT = (10 / 27, 11 / 27)
 
 
@@ -305,7 +306,7 @@
 
 def pieces_of(widths, cuts):
     found = []
-    for part in range(3):
+    for part in range(len(cuts) - 1):
         base = 0
         for weight, width in enumerate(widths):
             lo = max(base, cuts[part])
@@ -323,7 +324,8 @@
         self.shards, self.widths = shards, widths
         self.by_pairs = len(scratch) == 4
         self.whole = scratch[0]
-        self.bufs = [scratch[0].at[part] for part in range(3)] if self.by_pairs else scratch[:3]
+        self.bufs = [scratch[0].at[part] for part in range(3)] if self.by_pairs else scratch[:-3]
+        self.parts = range(len(orders))
         self.send, self.recv, self.local = scratch[-3:]
         self.near = {
             "up": (row_of(z + 1, y, core), x),
@@ -343,7 +345,7 @@
         if by_pairs:
             bufs = [pltpu.VMEM((3, 2, 16, rows, 3 * PAIR), bf16)]
         else:
-            bufs = [pltpu.VMEM((2, 16, rows, cuts[i + 1] - cuts[i]), bf16) for i in range(3)]
+            bufs = [pltpu.VMEM((2, 16, rows, cuts[i + 1] - cuts[i]), bf16) for i in range(len(cuts) - 1)]
         return bufs + [
             dma((3, 5)),
             dma((3, 17)),
@@ -384,14 +386,14 @@
             blocks, blocks, self.send.at[part, WAYS.index(way)], self.recv.at[part, 16], self.near[way]
         )
 
-    def each(self, step, act, parts=(0, 1, 2)):
-        for part in parts:
+    def each(self, step, act, parts=None):
+        for part in self.parts if parts is None else parts:
             for dz, dy, dx, onward in self.trees[part].get(step, []):
                 bz, by, bx = self.z + dz, (self.y + dy) % 2, (self.x + dx) % 2
                 cond = None if dz == 0 else ((bz >= 0) & (bz <= DEPTH - 1))
                 maybe(cond, lambda: act(part, bz, by, bx, onward))
 
-    def forward(self, step, parts=(0, 1, 2)):
+    def forward(self, step, parts=None):
         def act(part, bz, by, bx, onward):
             if step:
                 self.copy(part, bz, by, bx, "y").wait_recv()
@@ -400,12 +402,12 @@
 
         self.each(step, act, parts)
 
-    def arrive(self, parts=(0, 1, 2)):
-        for part in parts:
+    def arrive(self, parts=None):
+        for part in self.parts if parts is None else parts:
             self.all_of(part, 16, "core").wait_recv()
 
     def drain(self):
-        for part in range(3):
+        for part in self.parts:
             count = 1
             for axis in self.orders[part]:
                 if axis == "z":
@@ -464,12 +466,12 @@
     place = my_place()
     z, y, core, x = place
     one, two, three = (
-        Gatherer(place, shards, *shape["groups"][i], scr[6 * i - 2 * (i > 0) : 6 * i + 4])
+        Gatherer(place, shards, *shape["groups"][i], scr[shape["at"][i] : shape["at"][i + 1]])
         for i, shards in enumerate(([w_qkv], [w_out, w_fc], [w_proj]))
     )
     (
-        xm, xo, cm, xf, n1, pk, big, ib, att, bias, mid, n2, shifts, s_x, r_x, s_c, r_c, s_v, r_v, s_in, s_pair, s_end,
-    ) = scr[16:-9]
+        xm, xo, cm, xf, n1, pk, big, ib, att, bias, mid, n2, shifts, n1t, s_x, r_x, s_c, r_c, s_v, r_v, s_in, s_pair, s_end,
+    ) = scr[shape["at"][3] : -9]
     vec_o = scr[-9:]
     length, half_width = xm.shape
     width = 2 * half_width
@@ -478,7 +480,7 @@
     to_x = one.near["x"]
 
     def x_copy(i):
-        span = pl.ds(i * ROWS, ROWS)
+        span = pl.ds(pl.multiple_of(i * ROWS, ROWS), ROWS)
         return remote(x_in.at[1 - x, span], xo.at[span], s_x.at[i], r_x.at[i], to_x)
 
     own_cols = pl.ds(pl.multiple_of(x * half_width, PAIR), half_width)
@@ -506,11 +508,14 @@
     begin([x_copy(i) for i in range(blocks)])
     for part in range(2):
         bias[part] = half_bias(starts[x, 0, part], kinds[x, 0, part], part, half)
-    one.forward(1)
+    one.forward(1, (0,))
+    one.forward(1, (1,))
     end(two.loads())
     end(three.loads())
-    one.forward(2)
-    two.forward(0)
+    one.forward(2, (0,))
+    one.forward(1, (2,))
+    one.forward(2, (1,))
+    one.forward(3, (0,))
     end(vec_copies)
     is_low = x == 0
     full = []
@@ -529,24 +534,26 @@
         return ((value - average) * inverse * o_vec[:, full[gain]] + o_vec[:, full[shift]]).astype(bf16)
 
     def first_norm(i):
-        span = slice(i * ROWS, (i + 1) * ROWS)
+        span = pl.ds(pl.multiple_of(i * ROWS, ROWS), ROWS)
         x_copy(i).wait_recv()
         mine, other = xm[span, :], xo[span, :]
         xf[span, :half_width] = jnp.where(is_low, mine, other)
         xf[span, half_width:] = jnp.where(is_low, other, mine)
         n1[span, :] = norm(xf[span, :].astype(f32), 0, 1)
 
-    one.forward(3)
+    one.forward(2, (2,))
+    one.forward(3, (1,))
+    two.forward(0)
+    one.forward(4, (0,))
     first_norm(0)
-    first_norm(1)
-    one.forward(4)
-    first_norm(2)
-    one.forward(5)
-    first_norm(3)
+    one.forward(3, (2,))
+    one.forward(4, (1,))
+    one.forward(5, (0,))
     two.forward(1)
+    lax.fori_loop(1, blocks, lambda i, carry: (first_norm(i), carry)[1], 0)
     to_x_out = pltpu.make_async_copy(xf, o_x, s_end.at[0])
-    to_normed = pltpu.make_async_copy(n1, o_normed, s_end.at[1])
-    begin([to_x_out, to_normed])
+    to_normed = pltpu.make_async_copy(n1t, o_normed, s_end.at[1])
+    to_x_out.start()
 
     def pair_puts(j, step):
         wide = pl.ds(pl.multiple_of(3 * PAIR * j, PAIR), 3 * PAIR)
@@ -559,32 +566,37 @@
         ]
 
     def serve_0():
+        one.forward(5, (1,))
+        one.forward(4, (2,))
         two.forward(2)
+
+    def serve_1():
+        one.forward(5, (2,))
+        two.forward(3)
         one.arrive((1,))
-
-    def serve_1():
-        two.forward(3)
-        three.forward(0)
+        n1t[...] = n1[...].T
+        to_normed.start()
 
     def serve_2():
         two.forward(4)
-        cot_copy(0).start()
-        one.arrive((2,))
-        begin(one.stores([o_qkv]))
+        three.forward(0)
 
     def serve_3():
         two.forward(5)
         three.forward(1)
+        one.arrive((2,))
+        begin(one.stores([o_qkv]))
+        cot_copy(0).start()
+
+    def serve_4():
+        three.forward(2)
         cot_copy(1).start()
         own_cot.wait()
         put_cot.start()
 
-    def serve_4():
-        three.forward(2)
-        cot_copy(2).start()
-
     def serve_5():
         three.forward(3)
+        cot_copy(2).start()
         cot_copy(3).start()
 
     serves = (serve_0, serve_1, serve_2, serve_3, serve_4, serve_5)
@@ -635,12 +647,13 @@
     three.forward(4)
     ff_half = two.widths[1]
     puts = []
-    for k, ((part, _, at, src, w), side) in enumerate([(p, side) for p in fc_pieces for side in range(2)]):
-        cols = slice(side * ff_half + src, side * ff_half + src + w)
-        b_cols = slice(full[7].start + cols.start, full[7].start + cols.stop)
-
-        def block(i, carry):
+    for k, (part, _, at, src, w) in enumerate(fc_pieces):
+
+        def block(step, carry):
+            side, i = step // blocks, step % blocks
+            cols = pl.ds(pl.multiple_of(side * ff_half + src, PAIR), w)
             span = pl.ds(pl.multiple_of(i * ROWS, ROWS), ROWS)
+            b_cols = pl.ds(pl.multiple_of(full[7].start + side * ff_half + src, PAIR), w)
             hidden = nn(n2[span, :], two.weight(part, side, at, w)) + o_vec[:, b_cols]
             squared = hidden * hidden
             tanh = jnp.tanh(hidden * (GELU_A + (GELU_A * GELU_B) * squared))
@@ -651,14 +664,17 @@
             big[2 + i // 2, here, cols] = (gate + inner * (0.5 - 0.5 * tanh * tanh)).astype(bf16)
             return carry
 
-        lax.fori_loop(0, blocks, block, 0)
-        now = [
-            pltpu.make_async_copy(big.at[0:2, :, cols], o_active.at[:, :, cols], s_end.at[5 + 2 * k]),
-            pltpu.make_async_copy(big.at[2:4, :, cols], o_slope.at[:, :, cols], s_end.at[6 + 2 * k]),
-        ]
-        begin(now)
-        puts += now
-        if k == 1:
+        lax.fori_loop(0, 2 * blocks, block, 0)
+        for side in range(2):
+            cols = slice(side * ff_half + src, side * ff_half + src + w)
+            slot = 5 + 4 * k + 2 * side
+            now = [
+                pltpu.make_async_copy(big.at[0:2, :, cols], o_active.at[:, :, cols], s_end.at[slot]),
+                pltpu.make_async_copy(big.at[2:4, :, cols], o_slope.at[:, :, cols], s_end.at[slot + 1]),
+            ]
+            begin(now)
+            puts += now
+        if k == 0:
             three.forward(5)
     three.arrive()
     three_stores = three.stores([o_proj])
@@ -685,16 +701,17 @@
     pairs = width // PAIR
     groups = [
         (widths[:1], [0, 3 * PAIR, 6 * PAIR, 9 * PAIR], G0_ORDERS),
-        (widths[1:3], part_cuts(widths[1:3], *MIDDLE_CUT), REST_ORDERS),
+        (widths[1:3], part_cuts(widths[1:3], *MIDDLE_CUT), MIDDLE_ORDERS),
         (widths[3:], part_cuts(widths[3:], *GATHER_CUT), REST_ORDERS),
     ]
     ff = 2 * widths[2]
     sizes = [v.shape[0] for v in vectors]
-    shape = {"groups": groups, "vectors": sizes}
+    shape = {"groups": groups, "vectors": sizes, "at": [0]}
     dma = pltpu.SemaphoreType.DMA
     scratch = []
     for i, (_, cuts, _) in enumerate(groups):
         scratch += Gatherer.scratch_shapes(cuts, rows, i == 0)
+        shape["at"].append(len(scratch))
     scratch += [
         pltpu.VMEM((length, half_width), bf16),
         pltpu.VMEM((length, half_width), bf16),
@@ -709,6 +726,7 @@
         pltpu.VMEM((length, width), f32),
         pltpu.VMEM((length, width), bf16),
         pltpu.VMEM((pairs, 1, 3 * PAIR), f32),
+        pltpu.VMEM((width, length), bf16),
     ]
     scratch += [dma((4,)), dma((4,)), dma((4,)), dma((4,)), dma((9,)), dma((9,)), dma((3,)), dma((4,)), dma((17,))]
     scratch += [pltpu.VMEM((size,), f32) for size in sizes]
@@ -732,7 +750,7 @@
             out((pairs, half, 6 * half)),
             out((length, width), f32),
             out((length, width)),
-            out((length, width)),
+            out((width, length)),
             out((length, width), f32),
             out((length, width)),
             out((2, half, ff)),
@@ -1296,11 +1314,10 @@
     return outs, lax.psum(small, ("row", "col"))
 
 
-def part_cuts(widths, first, second):
+def part_cuts(widths, *shares):
     total = sum(widths) // 128
-    one = round(total * first)
-    two = round(total * (first + second))
-    return [0, one * 128, two * 128, total * 128]
+    ends = [round(total * sum(shares[: k + 1])) for k in range(len(shares))]
+    return [0] + [128 * end for end in ends] + [128 * total]
 
 
 def layer_norm(value):
@@ -1341,7 +1358,7 @@
         )
         qkv_all, out_all, fc_all, proj_all = weights
         ln1_gain, _, _, _, _, ln2_gain, _, _, b_proj = vectors
-        packed, p, inv, attended, normed_first, middle, normed_second, active, slope = saved
+        packed, p, inv, attended, normed_turned, middle, normed_second, active, slope = saved
         centred_second, inverse_second = layer_norm(middle)
     else:
         x_own = own_micro(x_in)
@@ -1395,7 +1412,7 @@
     if near:
         flat = jnp.concatenate(small).reshape(-1, 128)
         *outs, summed, grad_input = back_near(
-            [g_out, g_fc, g_proj], packed, attended, p, inv, grad_attended, normed_first.T, qkv_all,
+            [g_out, g_fc, g_proj], packed, attended, p, inv, grad_attended, normed_turned, qkv_all,
             x_own, grad_middle, ln1_gain, flat, shard,
         )
         outs[0] = outs[0].transpose(1, 0, 2)

time: 250 us -> 247 us (0.988); the launches traced: 246 us -> 247 us
    pallas_call x1, Pallas kernels: 95.2 us -> 98.1 us  [front_near(): pl.pallas_call(lambda *refs: front_kernel(shape, *refs), in_specs=[any_sp...]
  transfers between devices with their start and end apart: 1 -> 1, of which waited for: 0 -> 0; matrix products, arithmetic and copies ran while one was open for 17% -> 16% of each run, Pallas kernels for 36% -> 35%
where the time goes in v1:
time: 247 us
  Pallas kernels  185 us (75%)
  matrix products  44.3 us (18%)
  local copies, waits for them, and re-layouts  9.85 us (4%)
  other arithmetic  5.06 us (2%)
    pallas_call x1, Pallas kernels, front_near(): pl.pallas_call(lambda *refs: front_kernel(shape, *refs), in_specs=[any_sp...  98.1 us
    pallas_call x1, Pallas kernels, back_near(): pl.pallas_call(lambda *refs: back_kernel(shape, *refs), in_specs=[any_spa...  87.4 us
    dot_general x2, matrix products, nt(): lax.dot_general(a, b, (((1,), (1,)), ((), ())), preferred_element_type=f32)  18 us
    dot_general x3, matrix products, tn(): lax.dot_general(a, b, (((0,), (0,)), ((), ())), preferred_element_type=f32)  16.6 us
    dot_general x2, matrix products, nn(): lax.dot_general(a, b, (((1,), (0,)), ((), ())), preferred_element_type=f32)  9.61 us
  transfers between devices with their start and end apart: 1, of which 0 were waited for; matrix products, arithmetic and copies ran while one was open for 16% of the time, Pallas kernels for 35%

profile of v1, /device:TPU:0, one launch (start us, length us, event | category | flops | bytes accessed | tf_op | source)
XLA Modules:
  0.0 246.8 jit_solution(3723611020870009472)
XLA Ops:
  0.7 98.1 %gather_weights.1 = (bf16[16,48,2304]{2,1,0:T(8,128)(2,1)}, bf16[16,48,768]{2,1,0:T(8,128)(2,1)}, bf16[16,48,3072]{2,1,0:T(8,128)(2,1)}, bf16[16,48,3072]{2,1,0:...) custom-call(bf16[3,48,384]{2,1,0:T(8,128)(2,1)} %bitcast.41, ...), custom_call_target="tpu_custom_call" | custom-call | flops 21474836480 | bytes 209715200 | tf_op jit(solution)/shard_map/gather_weights/pallas_call | solution.py:740
  98.7 1.3 slice_reduce_fusion
  100.0 10.1 %add_convert_fusion = bf16[1024,768]{1,0:T(8,128)(2,1)S(1)} fusion(f32[1024,768]{1,0:T(8,128)} %get-tuple-element.37, bf16[1024,3072]{1,0:T(8,128)(2,1)} %bitcast.46, bf16[768,3072]{1,0:T(8,128)(2,1)} %bitcast.54, f32[768]{0:T(1024)S(1)} %get-tuple-element.66), kind=kOutput, calls=%fused_computation.11 | convolution fusion | flops 4834197504 | bytes 15731712 | tf_op jit(solution)/shard_map/dot_general | solution.py:25
  110.2 1.0 constant_dynamic-slice_fusion
  111.2 1.1 collective-permute-start
  112.3 0.4 multiply_reduce_fusion.2
  112.8 7.0 %convolution_convert_fusion = bf16[768,3072]{1,0:T(8,128)(2,1)} fusion(bf16[1024,768]{1,0:T(8,128)(2,1)S(1)} %copy-done.4, bf16[1024,3072]{1,0:T(8,128)(2,1)S(1)} %bitcast.49), kind=kOutput, calls=%fused_computation.3 | convolution fusion | flops 4834197504 | bytes 12582912 | tf_op jit(solution)/shard_map/dot_general | solution.py:29
  119.9 7.0 %convert_reduce_fusion = (f32[3072]{0:T(1024)S(1)}, bf16[1024,3072]{1,0:T(8,128)(2,1)}) fusion(bf16[1024,3072]{1,0:T(8,128)(2,1)S(1)} %bitcast.45, bf16[1024,768]{1,0:T(8,128)(2,1)S(1)} %copy-done.4, bf16[768,3072]{1,0:T(8,128)(2,1)S(1)} %bitcast.57), kind=kOutput, calls=%fused_computation.2 | convolution fusion | flops 4847563776 | bytes 18886656 | tf_op jit(solution)/shard_map/dot_general | solution.py:21
  127.0 7.9 %multiply_reduce_fusion = (f32[768]{0:T(1024)S(1)}, f32[1024]{0:T(1024)S(1)}, f32[1024]{0:T(1024)S(1)}, f32[768]{0:T(1024)S(1)}, f32[1024,768]{1,0:T(8,128)S(1)}) fusion(f32[1024,768]{1,0:T(8,128)S(1)} %copy-done, f32[1024]{0:T(1024)S(1)} %get-tuple-element.82, f32[1024]{0:T(1024)S(1)} %get-tuple-element.81, f32[768]{0:T(1024)S(1)} %get-tuple-element.65, ...), kind=kOutput, calls=%fused_computation.7 | convolution fusion | flops 4838912000 | bytes 17327104 | tf_op jit(solution)/shard_map/dot_general | solution.py:25
  134.9 1.5 fusion.3
  136.5 2.6 %convolution_convert_fusion.2.refs_7_ = bf16[1024,768]{1,0:T(8,128)(2,1)} fusion(bf16[768,768]{1,0:T(8,128)(2,1)S(1)} %bitcast.60, f32[1024,768]{1,0:T(8,128)S(1)} %get-tuple-element.68.refs_11_), kind=kOutput, calls=%fused_computation.13 | convolution fusion | flops 1209532416 | bytes 5898240 | tf_op jit(solution)/shard_map/dot_general | solution.py:21
  139.1 2.5 %convolution_convert_fusion.3 = bf16[768,768]{1,0:T(8,128)(2,1)} fusion(bf16[1024,768]{1,0:T(8,128)(2,1)S(1)} %copy-done.11, f32[1024,768]{1,0:T(8,128)S(1)} %get-tuple-element.68.refs_11_), kind=kOutput, calls=%fused_computation.15 | convolution fusion | flops 1209335808 | bytes 5898240 | tf_op jit(solution)/shard_map/dot_general | solution.py:29
  141.6 7.1 %convolution_convert_fusion.1 = bf16[768,3072]{1,0:T(8,128)(2,1)} fusion(bf16[1024,768]{1,0:T(8,128)(2,1)S(1)} %copy-done.12, bf16[1024,3072]{1,0:T(8,128)(2,1)S(1)} %bitcast.63), kind=kOutput, calls=%fused_computation.4 | convolution fusion | flops 4834197504 | bytes 12582912 | tf_op jit(solution)/shard_map/dot_general | solution.py:29
  148.8 0.6 copy-done.9
  149.4 87.4 %reduce_grads.1 = (f32[3,48,384]{2,1,0:T(8,128)}, f32[48,384]{1,0:T(8,128)}, f32[48,1536]{1,0:T(8,128)}, f32[48,1536]{1,0:T(8,128)}, f32[72,128]{1,0:T(8,128)}, /*index=5*/bf16[2,1024,384]{2,1,0:T(8,128)(2,1)}) custom-call(bf16[4,2,2,48,768]{4,3,2,1,0:T(8,128)(2,1)} %bitcast.61, bf16[4,2,2,48,3072]{4,3,2,1,0:T(8,128)(2,1)} %bitcast.58, ...), custom_call_target="tpu_custom_call" | custom-call | flops 32212254720 | bytes 209715200 | tf_op jit(solution)/shard_map/reduce_grads/pallas_call | solution.py:1284
  236.8 1.4 dynamic_slice.42
  238.2 1.5 fusion.4
  239.7 1.8 select_bitcast_fusion.1
  241.6 1.3 pad_maximum_fusion
  242.9 1.1 copy.42
  244.0 0.7 copy.43
  244.7 0.6 copy.44
  245.4 0.7 copy.45
  246.1 0.7 copy.46
  (59 shorter events, 0.2 us)
Async XLA Ops:
  100.0 12.7 %slice-start.2 = ((s8[6291456]{0:T(1024)(128)(4,1)}), s8[4194304]{0:T(1024)(128)(4,1)S(1)}, s32[]{:S(2)}) async-start(s8[6291456]{0:T(1024)(128)(4,1)} %bitcast.47), calls=%async_computation.2 | async-start | bytes 8388608
  100.0 12.3 %copy-start = (f32[1024,768]{1,0:T(8,128)S(1)}, f32[1024,768]{1,0:T(8,128)}, u32[]{:S(2)}) copy-start(f32[1024,768]{1,0:T(8,128)} %get-tuple-element.37) | copy-start | bytes 9437188
  100.0 12.7 %slice-start.3 = ((s8[6291456]{0:T(1024)(128)(4,1)}), s8[2097152]{0:T(1024)(128)(4,1)S(1)}, s32[]{:S(2)}) async-start(s8[6291456]{0:T(1024)(128)(4,1)} %bitcast.47), calls=%async_computation.3 | async-start | bytes 4194304
  110.2 9.7 %copy-start.3 = (bf16[1024,768]{1,0:T(8,128)(2,1)}, bf16[1024,768]{1,0:T(8,128)(2,1)S(1)}, u32[]{:S(2)}) copy-start(bf16[1024,768]{1,0:T(8,128)(2,1)S(1)} %add_convert_fusion) | copy-start | bytes 4718596
  110.2 2.6 %copy-start.4 = (bf16[1024,768]{1,0:T(8,128)(2,1)S(1)}, bf16[1024,768]{1,0:T(8,128)(2,1)}, u32[]{:S(2)}) copy-start(bf16[1024,768]{1,0:T(8,128)(2,1)} %get-tuple-element.41) | copy-start | bytes 4718596
  111.2 128.6 %collective-permute-start = (bf16[1024,384]{1,0:T(8,128)(2,1)}, bf16[1024,384]{1,0:T(8,128)(2,1)}, u32[]{:S(2)}, u32[]{:S(2)}) collective-permute-start(bf16[1024,384]{1,0:T(8,128)(2,1)} %constant_dynamic-slice_fusion), channel_id=1, source_target_pairs={{0,1},{1,0},{2,3},{3,2},{4,5},{5,4},{6,7},{7,6},{8,9},{9,8},{10,11... | collective-permute-start | bytes 2359304 | tf_op jit(solution)/shard_map/ppermute | solution.py:203
  112.3 7.5 %slice-start = ((s8[6291456]{0:T(1024)(128)(4,1)}), s8[4194304]{0:T(1024)(128)(4,1)S(1)}, s32[]{:S(2)}) async-start(s8[6291456]{0:T(1024)(128)(4,1)} %bitcast.43), calls=%async_computation | async-start | bytes 8388608
  112.3 7.5 %slice-start.6 = ((s8[4718592]{0:T(1024)(128)(4,1)}), s8[4194304]{0:T(1024)(128)(4,1)S(1)}, s32[]{:S(2)}) async-start(s8[4718592]{0:T(1024)(128)(4,1)} %bitcast.55), calls=%async_computation.6 | async-start | bytes 8388608
  112.8 7.1 %slice-start.1 = ((s8[6291456]{0:T(1024)(128)(4,1)}), s8[2097152]{0:T(1024)(128)(4,1)S(1)}, s32[]{:S(2)}) async-start(s8[6291456]{0:T(1024)(128)(4,1)} %bitcast.43), calls=%async_computation.1 | async-start | bytes 4194304
  112.8 7.1 %slice-start.7 = ((s8[4718592]{0:T(1024)(128)(4,1)}), s8[524288]{0:T(1024)(128)(4,1)S(1)}, s32[]{:S(2)}) async-start(s8[4718592]{0:T(1024)(128)(4,1)} %bitcast.55), calls=%async_computation.7 | async-start | bytes 1048576
  112.8 14.2 %slice-start.4 = ((s8[4718592]{0:T(1024)(128)(4,1)}), s8[524288]{0:T(1024)(128)(4,1)S(1)}, s32[]{:S(2)}) async-start(s8[4718592]{0:T(1024)(128)(4,1)} %bitcast.51), calls=%async_computation.4 | async-start | bytes 1048576
  119.9 7.1 %slice-start.5 = ((s8[4718592]{0:T(1024)(128)(4,1)}), s8[4194304]{0:T(1024)(128)(4,1)S(1)}, s32[]{:S(2)}) async-start(s8[4718592]{0:T(1024)(128)(4,1)} %bitcast.51), calls=%async_computation.5 | async-start | bytes 8388608
  134.9 1.6 copy-start.10
  134.9 6.7 %slice-start.8 = ((s8[6291456]{0:T(1024)(128)(4,1)}), s8[4194304]{0:T(1024)(128)(4,1)S(1)}, s32[]{:S(2)}) async-start(s8[6291456]{0:T(1024)(128)(4,1)} %bitcast.62), calls=%async_computation.8 | async-start | bytes 8388608
  136.4 2.6 %copy-start.1 = (f32[1024,768]{1,0:T(8,128)}, f32[1024,768]{1,0:T(8,128)S(1)}, u32[]{:S(2)}) copy-start(f32[1024,768]{1,0:T(8,128)S(1)} %get-tuple-element.68.refs_11_) | copy-start | bytes 9437188
  136.5 2.7 %copy-start.11 = (bf16[1024,768]{1,0:T(8,128)(2,1)S(1)}, bf16[1024,768]{1,0:T(8,128)(2,1)}, u32[]{:S(2)}) copy-start(bf16[1024,768]{1,0:T(8,128)(2,1)} %get-tuple-element.44.refs_4_) | copy-start | bytes 4718596
  136.5 5.2 %slice-start.9 = ((s8[6291456]{0:T(1024)(128)(4,1)}), s8[2097152]{0:T(1024)(128)(4,1)S(1)}, s32[]{:S(2)}) async-start(s8[6291456]{0:T(1024)(128)(4,1)} %bitcast.62), calls=%async_computation.9 | async-start | bytes 4194304
  139.1 2.5 %copy-start.12 = (bf16[1024,768]{1,0:T(8,128)(2,1)S(1)}, bf16[1024,768]{1,0:T(8,128)(2,1)}, u32[]{:S(2)}) copy-start(bf16[1024,768]{1,0:T(8,128)(2,1)} %get-tuple-element.45) | copy-start | bytes 4718596
  148.8 0.6 copy-start.9
  239.7 3.2 %copy-start.2 = (bf16[2,1024,384]{2,1,0:T(8,128)(2,1)S(1)}, bf16[2,1024,384]{2,1,0:T(8,128)(2,1)}, u32[]{:S(2)}) copy-start(bf16[2,1024,384]{2,1,0:T(8,128)(2,1)} %get-tuple-element.104) | copy-start | bytes 4718596
  241.5 2.5 %copy-start.7 = (f32[3,48,384]{2,1,0:T(8,128)S(1)}, f32[3,48,384]{2,1,0:T(8,128)}, u32[]{:S(2)}) copy-start(f32[3,48,384]{2,1,0:T(8,128)} %get-tuple-element.55) | copy-start | bytes 663556
  241.5 3.2 %copy-start.8 = (f32[48,384]{1,0:T(8,128)S(1)}, f32[48,384]{1,0:T(8,128)}, u32[]{:S(2)}) copy-start(f32[48,384]{1,0:T(8,128)} %get-tuple-element.56) | copy-start | bytes 221188
  241.6 3.8 %copy-start.6 = (f32[48,1536]{1,0:T(8,128)S(1)}, f32[48,1536]{1,0:T(8,128)}, u32[]{:S(2)}) copy-start(f32[48,1536]{1,0:T(8,128)} %get-tuple-element.114) | copy-start | bytes 884740
  241.6 4.5 %copy-start.5 = (f32[48,1536]{1,0:T(8,128)S(1)}, f32[48,1536]{1,0:T(8,128)}, u32[]{:S(2)}) copy-start(f32[48,1536]{1,0:T(8,128)} %get-tuple-element.58) | copy-start | bytes 884740
